TPU v7x, 32 devices: a whole 2x2x4 slice. The times are simulated.
32 devices in a mesh: groups: 2 (over x), tm: 16 (over z, y, core).
Axes of the slice: x: 2, y: 2, z: 4, core: 2. Of those that a mesh axis runs over, the one named last changes fastest.
Arguments:
- token_ids: int32 [4096, 8], P(('groups', 'tm')), parts along dimension 0, may hold values from 0 to 127
- field_offsets: int32 [16], P('groups'), parts along dimension 0, may hold values from 0 to 896
- embed_table: bfloat16 [1024, 1024], replicated, may hold values from -2.09375 to 2.09375
- w_in: bfloat16 [1024, 3072], P('tm'), may hold values from -0.1875 to 0.1875
- short_taps: float32 [3, 3072], replicated, may hold values from -1 to 1
- filters: bfloat16 [2, 1024, 2048], P(None, 'tm'), may hold values from -1.1 to 1.1
- cotangent: bfloat16 [4096, 1024], P(('groups', 'tm')), parts along dimension 0, may hold values from -0.125 to 0.125
Outputs:
- mixer_out: bfloat16 [4096, 1024], P(('groups', 'tm')), parts along dimension 0
- weight_grads: float32 [2048, 3072], P(('groups', 'tm')), parts along dimension 0
- tap_grads: float32 [6, 3072], P('groups'), parts along dimension 0
- filter_grads: float32 [4, 1024, 2048], P('groups', 'tm'), parts along dimension 0
There are 2 independent parts, one for each index of `groups`. A program takes and returns all parts, laid end to end along the dimension named above; an argument that names none is the same for every part. Nothing has to cross between parts.
All inputs are finite; a program needn't handle non-finite values.
Results may differ from a plain program's by a relative error of at most 0.035.
Values may be sent and summed in bfloat16 or wider, within the bound.
A program may use at most 128 MiB of HBM per device.

v0:
```python
import math

import jax
import jax.numpy as jnp
from jax import lax
from jax.sharding import PartitionSpec as P

HIGHEST = lax.Precision.HIGHEST


def shifted(value, axis, steps):
    count = lax.axis_size(axis)
    initial, last = (max(0, -steps), min(count, count - steps))
    return lax.ppermute(value, axis, [(source, source + steps) for source in range(initial, last)])


def cis_tables(count_a, count_b, modulus):
    left = jnp.arange(count_a, dtype=jnp.int32)[:, None]
    right = jnp.arange(count_b, dtype=jnp.int32)[None, :]
    angle = 2.0 * math.pi / modulus * (left * right % modulus).astype(jnp.float32)
    return (jnp.cos(angle), jnp.sin(angle))


def build_tables(first_len, second_len, total):
    first_cos, first_sin = cis_tables(first_len, first_len // 2, first_len)
    twist_cos, twist_sin = cis_tables(first_len, second_len, total)
    second_cos, second_sin = cis_tables(second_len, second_len, second_len)
    first_both = jnp.concatenate([first_cos, -first_sin], axis=0)
    forward_second = jnp.concatenate(
        [
            jnp.concatenate([second_cos, -second_sin], axis=1),
            jnp.concatenate([second_sin, second_cos], axis=1),
        ],
        axis=0,
    )
    inverse_second = jnp.concatenate(
        [
            jnp.concatenate([second_cos, second_sin], axis=1),
            jnp.concatenate([-second_sin, second_cos], axis=1),
        ],
        axis=0,
    )
    return (first_both, twist_cos, twist_sin, forward_second, inverse_second)


def spectrum(series, tables):
    first_both, twist_cos, twist_sin, forward_second, inverse_second = tables
    channels, length = series.shape
    rows_k = twist_cos.shape[0]
    half = first_both.shape[1]
    second_len = twist_cos.shape[1]
    blocks = series.reshape(channels, half, length // half)
    part = jnp.einsum("ka,cab->ckb", first_both, blocks, precision=HIGHEST)
    part_re = part[:, :rows_k]
    part_im = part[:, rows_k:]
    turn_re = part_re * twist_cos + part_im * twist_sin
    turn_im = part_im * twist_cos - part_re * twist_sin
    turned = jnp.concatenate([turn_re, turn_im], axis=2)
    result = jnp.einsum("ckb,bm->ckm", turned, forward_second, precision=HIGHEST)
    return (result[:, :, :second_len], result[:, :, second_len:])


def signal_of(pair, tables):
    first_both, twist_cos, twist_sin, forward_second, inverse_second = tables
    spec_re, spec_im = pair
    channels = spec_re.shape[0]
    second_len = twist_cos.shape[1]
    total = twist_cos.shape[0] * second_len
    joined = jnp.concatenate([spec_re, spec_im], axis=2)
    back = jnp.einsum("ckm,mb->ckb", joined, inverse_second, precision=HIGHEST)
    back_re = back[:, :, :second_len]
    back_im = back[:, :, second_len:]
    turn_re = back_re * twist_cos - back_im * twist_sin
    turn_im = back_im * twist_cos + back_re * twist_sin
    turned = jnp.concatenate([turn_re, turn_im], axis=1)
    blocks = jnp.einsum("ka,ckb->cab", first_both, turned, precision=HIGHEST)
    return blocks.reshape(channels, -1) * (1.0 / total)


def product(left, right, conjugate):
    left_re, left_im = left
    right_re, right_im = right
    if conjugate:
        right_im = -right_im
    return (left_re * right_re - left_im * right_im, left_re * right_im + left_im * right_re)


def widen(array):
    return array.astype(jnp.float32)


def local(token_ids, field_offsets, embed_table, w_in, short_taps, filters, cotangent):
    tok_rows, width = cotangent.shape
    peers = lax.axis_size("tm")
    row_index = token_ids + field_offsets[None, :]
    embedded = jnp.sum(jnp.take(embed_table, row_index, axis=0).astype(jnp.float32), axis=1).astype(
        jnp.bfloat16
    )
    block = embedded
    proj = jnp.dot(
        block, lax.all_gather(w_in, "tm", axis=0, tiled=True), preferred_element_type=jnp.float32
    ).astype(jnp.bfloat16)
    before = shifted(proj[tok_rows - 2 :], "tm", 1)
    padded = jnp.concatenate([widen(before), widen(proj)], axis=0)
    mixed = (
        short_taps[0] * padded[2:]
        + short_taps[1] * padded[1 : tok_rows + 1]
        + short_taps[2] * padded[:tok_rows]
    ).astype(jnp.bfloat16)
    values = mixed[:, :width]
    first_gate = mixed[:, width : 2 * width]
    second_gate = mixed[:, 2 * width :]
    total = 2 * tok_rows * peers
    bits = total.bit_length() - 1
    first_len = 1 << (bits + 1) // 2
    second_len = total // first_len
    tables = build_tables(first_len, second_len, total)
    first_spec = spectrum(widen(filters[0]), tables)
    second_spec = spectrum(widen(filters[1]), tables)

    def split_time(series):
        return series.reshape(tok_rows, peers, -1)

    def channel_major(moved):
        return moved.reshape(moved.shape[0], -1).T

    def time_major(block):
        return block.T.reshape(block.shape[1], 1, block.shape[0])

    def to_channels(series):
        moved = lax.all_to_all(split_time(series), "tm", split_axis=1, concat_axis=0, tiled=True)
        return channel_major(moved)

    def to_time(block):
        moved = lax.all_to_all(time_major(block), "tm", split_axis=0, concat_axis=1, tiled=True)
        return moved.reshape(tok_rows, -1)

    value_spec = spectrum(widen(to_channels(values)), tables)
    first_conv = to_time(
        signal_of(product(value_spec, first_spec, False), tables).astype(jnp.bfloat16)
    )
    first_mix = (widen(first_gate) * widen(first_conv)).astype(jnp.bfloat16)
    mix_spec = spectrum(widen(to_channels(first_mix)), tables)
    second_conv = to_time(
        signal_of(product(mix_spec, second_spec, False), tables).astype(jnp.bfloat16)
    )
    mixer_out = (widen(second_gate) * widen(second_conv)).astype(jnp.bfloat16)
    upstream = widen(cotangent)
    grad_conv2 = (upstream * widen(second_gate)).astype(jnp.bfloat16)
    grad_gate2 = (upstream * widen(second_conv)).astype(jnp.bfloat16)
    grad_spec2 = spectrum(widen(to_channels(grad_conv2)), tables)
    grad_mix = to_time(
        signal_of(product(grad_spec2, second_spec, True), tables).astype(jnp.bfloat16)
    )
    filter_two = signal_of(product(grad_spec2, mix_spec, True), tables)
    grad_gate1 = (widen(grad_mix) * widen(first_conv)).astype(jnp.bfloat16)
    grad_conv1 = (widen(grad_mix) * widen(first_gate)).astype(jnp.bfloat16)
    grad_spec1 = spectrum(widen(to_channels(grad_conv1)), tables)
    grad_values = to_time(
        signal_of(product(grad_spec1, first_spec, True), tables).astype(jnp.bfloat16)
    )
    filter_one = signal_of(product(grad_spec1, value_spec, True), tables)
    filter_grads = jnp.stack([filter_one, filter_two], axis=0)
    grad_mixed = jnp.concatenate([grad_values, grad_gate1, grad_gate2], axis=1)
    after = shifted(grad_mixed[:2], "tm", -1)
    grad_wide = widen(grad_mixed)
    grad_padded = jnp.concatenate([grad_wide, widen(after)], axis=0)
    grad_proj = (
        short_taps[0] * grad_wide
        + short_taps[1] * grad_padded[1 : tok_rows + 1]
        + short_taps[2] * grad_padded[2:]
    ).astype(jnp.bfloat16)
    tap_terms = jnp.stack(
        [
            jnp.sum(grad_wide * padded[2:], axis=0),
            jnp.sum(grad_wide * padded[1 : tok_rows + 1], axis=0),
            jnp.sum(grad_wide * padded[:tok_rows], axis=0),
        ],
        axis=0,
    )
    tap_grads = lax.psum(tap_terms, "tm")
    block = embedded
    weight_grads = lax.psum_scatter(
        jnp.einsum("tr,tc->rc", block, grad_proj, preferred_element_type=jnp.float32),
        "tm",
        scatter_dimension=0,
        tiled=True,
    )
    return (mixer_out, weight_grads, tap_grads, filter_grads)


def solution(mesh):
    return jax.shard_map(
        local,
        mesh=mesh,
        in_specs=(
            P(("groups", "tm"), None),
            P("groups"),
            P(),
            P("tm", None),
            P(),
            P(None, "tm", None),
            P(("groups", "tm"), None),
        ),
        out_specs=(
            P(("groups", "tm"), None),
            P(("groups", "tm"), None),
            P("groups", None),
            P("groups", "tm", None),
        ),
        check_vma=False,
    )
```

profile of v0, /device:TPU:9, one launch (start us, length us, event | category | flops | bytes accessed | tf_op | source)
XLA Modules:
  0.0 532.8 jit_solution(3606033595169535217)
XLA Ops:
  19.8 53.9 %all-gather.2.cloned.1.call-done = bf16[1024,3072]{1,0:T(8,128)(2,1)} async-done(((bf16[64,3072]{1,0:T(8,128)(2,1)}), bf16[1024,3072]{1,0:T(8,128)(2,1)}) %all-gather.2.cloned.1.call-update) | async-done | bytes 6291472 | tf_op jit(solution)/shard_map/all_gather | solution.py:101
  92.6 6.3 %all-to-all-done.4 = bf16[128,16,64]{0,2,1:T(8,128)(2,1)} async-done(((bf16[128,16,64]{0,2,1:T(8,128)(2,1)}), bf16[128,16,64]{0,2,1:T(8,128)(2,1)}, u32[]{:S(2)}, u32[]{:S(2)}) %all-to-all-start.4) | async-done | bytes 262176 | tf_op jit(solution)/shard_map/all_to_all | solution.py:131
  105.1 6.7 %fusion.16 = f32[64,64,128]{2,1,0:T(8,128)S(1)} fusion(f32[128,128,1]{1,0,2:T(8,128)S(1)} %get-tuple-element.57, f32[64,64,64]{1,2,0:T(8,128)S(1)} %get-tuple-element.36, f32[64,64,64]{1,2,0:T(8,128)S(1)} %get-tuple-element.35), kind=kOutput, calls=%fused_computation.17 | convolution fusion | flops 805830656 | bytes 4259840 | tf_op jit(solution)/shard_map/ckb,bm->ckm/dot_general | solution.py:59
  111.8 7.2 %fusion.12 = f32[64,64,128]{2,1,0:T(8,128)S(1)} fusion(f32[128,128,1]{1,0,2:T(8,128)S(1)} %get-tuple-element.57, f32[64,64,64]{1,2,0:T(8,128)S(1)} %get-tuple-element.69, f32[64,64,64]{1,2,0:T(8,128)S(1)} %get-tuple-element.70), kind=kOutput, calls=%fused_computation.13 | convolution fusion | flops 805830656 | bytes 4259840 | tf_op jit(solution)/shard_map/ckb,bm->ckm/dot_general | solution.py:59
  120.3 6.2 %fusion.40 = f32[64,64,128]{1,2,0:T(8,128)S(1)} fusion(f32[128,128,1]{1,0,2:T(8,128)S(1)} %get-tuple-element.58, f32[64,64,64]{2,1,0:T(8,128)S(1)} %get-tuple-element.28, f32[64,64,64]{2,1,0:T(8,128)S(1)} %get-tuple-element.27), kind=kOutput, calls=%fused_computation.42 | convolution fusion | flops 805830656 | bytes 4259840 | tf_op jit(solution)/shard_map/ckm,mb->ckb/dot_general | solution.py:70
  170.0 6.1 %all-to-all-start.6 = ((bf16[128,16,64]{0,2,1:T(8,128)(2,1)}), bf16[128,16,64]{0,2,1:T(8,128)(2,1)}, u32[]{:S(2)}, u32[]{:S(2)}) async-start(bf16[128,16,64]{0,2,1:T(8,128)(2,1)} %bitcast.197), calls=%async_computation.6 | async-start | bytes 524288 | tf_op jit(solution)/shard_map/all_to_all | solution.py:131
  198.4 6.7 %fusion.20 = f32[64,64,128]{2,1,0:T(8,128)S(1)} fusion(f32[128,128,1]{1,0,2:T(8,128)S(1)} %get-tuple-element.57, f32[64,64,64]{1,2,0:T(8,128)S(1)} %get-tuple-element.34, f32[64,64,64]{1,2,0:T(8,128)S(1)} %get-tuple-element.33), kind=kOutput, calls=%fused_computation.21 | convolution fusion | flops 805830656 | bytes 4259840 | tf_op jit(solution)/shard_map/ckb,bm->ckm/dot_general | solution.py:59
  205.1 7.1 %fusion.4 = f32[64,64,128]{2,1,0:T(8,128)S(1)} fusion(f32[128,128,1]{1,0,2:T(8,128)S(1)} %get-tuple-element.57, f32[64,64,64]{1,2,0:T(8,128)S(1)} %get-tuple-element.65, f32[64,64,64]{1,2,0:T(8,128)S(1)} %get-tuple-element.66), kind=kOutput, calls=%fused_computation.5 | convolution fusion | flops 805830656 | bytes 4259840 | tf_op jit(solution)/shard_map/ckb,bm->ckm/dot_general | solution.py:59
  212.2 6.7 %fusion = f32[64,64,128]{2,1,0:T(8,128)S(1)} fusion(f32[128,128,1]{1,0,2:T(8,128)S(1)} %get-tuple-element.57, f32[64,64,64]{1,2,0:T(8,128)S(1)} %get-tuple-element.67, f32[64,64,64]{1,2,0:T(8,128)S(1)} %get-tuple-element.68), kind=kOutput, calls=%fused_computation.1 | convolution fusion | flops 805830656 | bytes 4259840 | tf_op jit(solution)/shard_map/ckb,bm->ckm/dot_general | solution.py:59
  226.2 8.3 %fusion.48 = f32[64,64,128]{1,2,0:T(8,128)S(1)} fusion(f32[128,128,1]{1,0,2:T(8,128)S(1)} %get-tuple-element.58, f32[64,64,64]{2,1,0:T(8,128)} %get-tuple-element.26, f32[64,64,64]{2,1,0:T(8,128)} %get-tuple-element.25), kind=kOutput, calls=%fused_computation.50 | convolution fusion | flops 805830656 | bytes 4259840 | tf_op jit(solution)/shard_map/ckm,mb->ckb/dot_general | solution.py:70
  234.5 6.2 %fusion.56 = f32[64,64,128]{1,2,0:T(8,128)S(1)} fusion(f32[128,128,1]{1,0,2:T(8,128)S(1)} %get-tuple-element.58, f32[64,64,64]{2,1,0:T(8,128)S(1)} %copy-done.9, f32[64,64,64]{2,1,0:T(8,128)S(1)} %copy-done.8), kind=kOutput, calls=%fused_computation.58 | convolution fusion | flops 805830656 | bytes 4259840 | tf_op jit(solution)/shard_map/ckm,mb->ckb/dot_general | solution.py:70
  240.7 6.2 %fusion.24 = f32[64,64,128]{1,2,0:T(8,128)S(1)} fusion(f32[128,128,1]{1,0,2:T(8,128)S(1)} %get-tuple-element.58, f32[64,64,64]{2,1,0:T(8,128)S(1)} %get-tuple-element.45, f32[64,64,64]{2,1,0:T(8,128)S(1)} %get-tuple-element.46), kind=kOutput, calls=%fused_computation.26 | convolution fusion | flops 805830656 | bytes 4259840 | tf_op jit(solution)/shard_map/ckm,mb->ckb/dot_general | solution.py:70
  251.5 6.6 %fusion.125 = bf16[64,32,64]{2,1,0:T(8,128)(2,1)} fusion(f32[128,32,1]{0,1,2:T(8,128)S(1)} %maximum_bitcast_fusion, f32[64,64,64]{1,2,0:T(8,128)S(1)} %get-tuple-element.59, f32[64,64,64]{1,2,0:T(8,128)S(1)} %get-tuple-element.60), kind=kOutput, calls=%fused_computation.150 | convolution fusion | flops 202113024 | bytes 2375680 | tf_op jit(solution)/shard_map/ka,ckb->cab/dot_general | solution.py:76
  266.8 14.8 %all_to_all.102 = bf16[16,2,4096]{2,1,0:T(2,128)(2,1)} all-to-all(bf16[16,2,4096]{2,1,0:T(2,128)(2,1)} %reshape.212), channel_id=1, replica_groups=mesh['groups'=2,'tm'=16] {'tm'}, dimensions={0} | all-to-all | bytes 524288 | tf_op jit(solution)/shard_map/all_to_all | solution.py:135
  301.6 8.0 %fusion.116 = bf16[64,32,64]{2,1,0:T(8,128)(2,1)S(1)} fusion(f32[128,32,1]{0,1,2:T(8,128)S(1)} %maximum_bitcast_fusion, f32[64,64,64]{1,2,0:T(8,128)} %get-tuple-element.61, f32[64,64,64]{1,2,0:T(8,128)} %get-tuple-element.62), kind=kOutput, calls=%fused_computation.147 | convolution fusion | flops 202113024 | bytes 2375680 | tf_op jit(solution)/shard_map/ka,ckb->cab/dot_general | solution.py:76
  315.5 6.5 %all-to-all-start.7 = ((bf16[16,2,4096]{2,1,0:T(2,128)(2,1)}), bf16[16,2,4096]{2,1,0:T(2,128)(2,1)}, u32[]{:S(2)}, u32[]{:S(2)}) async-start(bf16[16,2,4096]{2,1,0:T(2,128)(2,1)} %reshape.218), calls=%async_computation.7 | async-start | bytes 524288 | tf_op jit(solution)/shard_map/all_to_all | solution.py:135
  327.4 6.7 %fusion.8 = f32[64,64,128]{2,1,0:T(8,128)S(1)} fusion(f32[128,128,1]{1,0,2:T(8,128)S(1)} %get-tuple-element.57, f32[64,64,64]{1,2,0:T(8,128)S(1)} %get-tuple-element.38, f32[64,64,64]{1,2,0:T(8,128)S(1)} %get-tuple-element.37), kind=kOutput, calls=%fused_computation.9 | convolution fusion | flops 805830656 | bytes 4259840 | tf_op jit(solution)/shard_map/ckb,bm->ckm/dot_general | solution.py:59
  337.3 8.0 %fusion.64 = f32[64,64,128]{1,2,0:T(8,128)S(1)} fusion(f32[128,128,1]{1,0,2:T(8,128)S(1)} %get-tuple-element.58, f32[64,64,64]{2,1,0:T(8,128)} %get-tuple-element.24, f32[64,64,64]{2,1,0:T(8,128)S(1)} %get-tuple-element.23), kind=kOutput, calls=%fused_computation.66 | convolution fusion | flops 805830656 | bytes 4259840 | tf_op jit(solution)/shard_map/ckm,mb->ckb/dot_general | solution.py:70
  345.3 6.2 %fusion.32 = f32[64,64,128]{1,2,0:T(8,128)S(1)} fusion(f32[128,128,1]{1,0,2:T(8,128)S(1)} %get-tuple-element.58, f32[64,64,64]{2,1,0:T(8,128)S(1)} %get-tuple-element.47, f32[64,64,64]{2,1,0:T(8,128)S(1)} %get-tuple-element.48), kind=kOutput, calls=%fused_computation.34 | convolution fusion | flops 805830656 | bytes 4259840 | tf_op jit(solution)/shard_map/ckm,mb->ckb/dot_general | solution.py:70
  386.4 6.4 %fusion.128 = f32[1024,3072]{1,0:T(8,128)} fusion(bf16[128,1024]{1,0:T(8,128)(2,1)S(1)} %copy-done.11, f32[128,3072]{1,0:T(8,128)S(1)} %get-tuple-element.50, f32[2,3072]{1,0:T(2,128)S(1)} %convert_element_type.300, f32[3072]{0:T(1024)S(1)} %bitcast.207, f32[3072]{0:T(1024)S(1)} %bitcast.209, f32[3072]{0:T(1024)S(1)} %bitcast.205), kind=kOutput, calls=%fused_computation.152 | convolution fusion | flops 808452096 | bytes 14479360 | tf_op jit(solution)/shard_map/tr,tc->rc/dot_general | solution.py:184
  394.5 7.4 %fusion.89 = f32[64,32,64]{2,1,0:T(8,128)S(1)} fusion(f32[128,32,1]{0,1,2:T(8,128)S(1)} %maximum_bitcast_fusion, f32[64,64,64]{1,2,0:T(8,128)} %get-tuple-element.10, f32[64,64,64]{1,2,0:T(8,128)S(1)} %copy-done.7), kind=kOutput, calls=%fused_computation.138 | convolution fusion | flops 201981952 | bytes 2637824 | tf_op jit(solution)/shard_map/ka,ckb->cab/dot_general | solution.py:76
  403.1 8.6 %fusion.83 = f32[64,32,64]{2,1,0:T(8,128)S(1)} fusion(f32[128,32,1]{0,1,2:T(8,128)S(1)} %maximum_bitcast_fusion, f32[64,64,64]{1,2,0:T(8,128)} %get-tuple-element.12, f32[64,64,64]{1,2,0:T(8,128)} %get-tuple-element.11), kind=kOutput, calls=%fused_computation.136 | convolution fusion | flops 201981952 | bytes 2637824 | tf_op jit(solution)/shard_map/ka,ckb->cab/dot_general | solution.py:76
  416.2 54.7 %psum.7 = f32[3,3072]{1,0:T(4,128)} all-reduce(f32[3,3072]{1,0:T(4,128)S(1)} %pad_maximum_fusion.8), channel_id=1, replica_groups=mesh['groups'=2,'tm'=16] {'tm'}, use_global_device_ids=true, to_apply=%region_5.6 | all-reduce | flops 9216 | bytes 73728 | tf_op jit(solution)/shard_map/psum | solution.py:181
  470.9 54.8 %reduce-scatter.2.cloned.1.call-done = f32[64,3072]{1,0:T(8,128)} async-done(((f32[1024,3072]{1,0:T(8,128)}), f32[64,3072]{1,0:T(8,128)}) %reduce-scatter.2.cloned.1.call-update) | async-done | bytes 786448 | tf_op jit(solution)/shard_map/reduce_scatter | solution.py:183
  (204 shorter events, 201.4 us)
Async XLA Ops:
  7.2 66.6 %all-gather.2.cloned.1.call-start = ((), (), s32[]{:S(2)}) async-start(), calls=%async_computation.9 | async-start | bytes 6684672 | tf_op jit(solution)/shard_map/all_gather | solution.py:101
  19.0 58.6 %copy-start.10 = (bf16[128,1024]{1,0:T(8,128)(2,1)}, bf16[128,1024]{1,0:T(8,128)(2,1)S(1)}, u32[]{:S(2)}) copy-start(bf16[128,1024]{1,0:T(8,128)(2,1)S(1)} %fusion.72) | copy-start | bytes 786436
  19.8 63.0 %copy-start.30 = (f32[1,3072]{1,0:T(1,128)}, f32[1,3072]{1,0:T(1,128)S(1)}, u32[]{:S(2)}) copy-start(f32[1,3072]{1,0:T(1,128)S(1)} %get-tuple-element.71) | copy-start | bytes 36868
  19.8 63.0 %copy-start.32 = (f32[1,3072]{1,0:T(1,128)}, f32[1,3072]{1,0:T(1,128)S(1)}, u32[]{:S(2)}) copy-start(f32[1,3072]{1,0:T(1,128)S(1)} %get-tuple-element.72) | copy-start | bytes 36868
  19.8 63.0 %copy-start.34 = (f32[1,3072]{1,0:T(1,128)}, f32[1,3072]{1,0:T(1,128)S(1)}, u32[]{:S(2)}) copy-start(f32[1,3072]{1,0:T(1,128)S(1)} %get-tuple-element.73) | copy-start | bytes 36868
  77.6 6.5 %copy-start.5 = (f32[128,3072]{1,0:T(8,128)}, f32[128,3072]{1,0:T(8,128)S(1)}, u32[]{:S(2)}) copy-start(f32[128,3072]{1,0:T(8,128)S(1)} %get-tuple-element.74) | copy-start | bytes 4718596
  77.6 6.4 %copy-start.25 = (bf16[128,1024]{1,0:T(8,128)(2,1)S(1)}, bf16[128,1024]{1,0:T(8,128)(2,1)}, u32[]{:S(2)}) copy-start(bf16[128,1024]{1,0:T(8,128)(2,1)} %param.13) | copy-start | bytes 786436
  78.5 4.3 collective-permute-start
  84.9 14.0 %all-to-all-start.4 = ((bf16[128,16,64]{0,2,1:T(8,128)(2,1)}), bf16[128,16,64]{0,2,1:T(8,128)(2,1)}, u32[]{:S(2)}, u32[]{:S(2)}) async-start(bf16[128,16,64]{0,2,1:T(8,128)(2,1)} %bitcast.31), calls=%async_computation.4 | async-start | bytes 524288 | tf_op jit(solution)/shard_map/all_to_all | solution.py:131
  139.9 13.5 %all-to-all-start.5 = ((bf16[16,2,4096]{2,1,0:T(2,128)(2,1)}), bf16[16,2,4096]{2,1,0:T(2,128)(2,1)S(1)}, u32[]{:S(2)}, u32[]{:S(2)}) async-start(bf16[16,2,4096]{2,1,0:T(2,128)(2,1)} %reshape.216), calls=%async_computation.5 | async-start | bytes 524288 | tf_op jit(solution)/shard_map/all_to_all | solution.py:135
  153.4 16.6 %all-to-all-start = ((bf16[128,16,64]{0,2,1:T(8,128)(2,1)}), bf16[128,16,64]{0,2,1:T(8,128)(2,1)}, u32[]{:S(2)}, u32[]{:S(2)}) async-start(bf16[128,16,64]{0,2,1:T(8,128)(2,1)} %bitcast.6), calls=%async_computation | async-start | bytes 524288 | tf_op jit(solution)/shard_map/all_to_all | solution.py:131
  170.0 17.4 %all-to-all-start.6 = ((bf16[128,16,64]{0,2,1:T(8,128)(2,1)}), bf16[128,16,64]{0,2,1:T(8,128)(2,1)}, u32[]{:S(2)}, u32[]{:S(2)}) async-start(bf16[128,16,64]{0,2,1:T(8,128)(2,1)} %bitcast.197), calls=%async_computation.6 | async-start | bytes 524288 | tf_op jit(solution)/shard_map/all_to_all | solution.py:131
  226.2 8.3 %copy-start.8 = (f32[64,64,64]{2,1,0:T(8,128)S(1)}, f32[64,64,64]{2,1,0:T(8,128)}, u32[]{:S(2)}) copy-start(f32[64,64,64]{2,1,0:T(8,128)} %get-tuple-element.21) | copy-start | bytes 3145732
  226.2 8.3 %copy-start.9 = (f32[64,64,64]{2,1,0:T(8,128)S(1)}, f32[64,64,64]{2,1,0:T(8,128)}, u32[]{:S(2)}) copy-start(f32[64,64,64]{2,1,0:T(8,128)} %get-tuple-element.22) | copy-start | bytes 3145732
  296.2 19.4 %all-to-all-start.2 = ((bf16[128,16,64]{0,2,1:T(8,128)(2,1)}), bf16[128,16,64]{0,2,1:T(8,128)(2,1)}, u32[]{:S(2)}, u32[]{:S(2)}) async-start(bf16[128,16,64]{0,2,1:T(8,128)(2,1)} %bitcast.20), calls=%async_computation.2 | async-start | bytes 524288 | tf_op jit(solution)/shard_map/all_to_all | solution.py:131
  315.5 47.9 %all-to-all-start.7 = ((bf16[16,2,4096]{2,1,0:T(2,128)(2,1)}), bf16[16,2,4096]{2,1,0:T(2,128)(2,1)}, u32[]{:S(2)}, u32[]{:S(2)}) async-start(bf16[16,2,4096]{2,1,0:T(2,128)(2,1)} %reshape.218), calls=%async_computation.7 | async-start | bytes 524288 | tf_op jit(solution)/shard_map/all_to_all | solution.py:135
  327.4 6.7 %copy-start.3 = (f32[64,64,128]{2,1,0:T(8,128)S(1)}, f32[64,64,128]{2,1,0:T(8,128)}, u32[]{:S(2)}) copy-start(f32[64,64,128]{2,1,0:T(8,128)} %copy-done.2) | copy-start | bytes 6291460
  363.4 14.7 %all-to-all-start.3 = ((bf16[16,2,4096]{2,1,0:T(2,128)(2,1)}), bf16[16,2,4096]{2,1,0:T(2,128)(2,1)S(1)}, u32[]{:S(2)}, u32[]{:S(2)}) async-start(bf16[16,2,4096]{2,1,0:T(2,128)(2,1)} %reshape.214), calls=%async_computation.3 | async-start | bytes 524288 | tf_op jit(solution)/shard_map/all_to_all | solution.py:135
  369.4 156.4 %reduce-scatter.2.cloned.1.call-start = ((), (), s32[]{:S(2)}) async-start(), calls=%async_computation.10 | async-start | bytes 13369344 | tf_op jit(solution)/shard_map/reduce_scatter | solution.py:183
  372.5 8.6 %copy-start.15 = (bf16[128,1024]{1,0:T(8,128)(2,1)}, bf16[128,1024]{1,0:T(8,128)(2,1)S(1)}, u32[]{:S(2)}) copy-start(bf16[128,1024]{1,0:T(8,128)(2,1)S(1)} %copy.256) | copy-start | bytes 786436
  380.3 6.1 %copy-start.35 = (f32[1,3072]{1,0:T(1,128)S(1)}, f32[1,3072]{1,0:T(1,128)}, u32[]{:S(2)}) copy-start(f32[1,3072]{1,0:T(1,128)} %copy-done.34) | copy-start | bytes 36868
  381.1 11.7 %copy-start.17 = (bf16[128,1024]{1,0:T(8,128)(2,1)}, bf16[128,1024]{1,0:T(8,128)(2,1)S(1)}, u32[]{:S(2)}) copy-start(bf16[128,1024]{1,0:T(8,128)(2,1)S(1)} %get-tuple-element.53) | copy-start | bytes 786436
  381.4 5.0 collective-permute-start.1
  412.9 112.9 %copy-start.1 = (bf16[1024,1024]{1,0:T(8,128)(2,1)S(1)}, bf16[1024,1024]{1,0:T(8,128)(2,1)}, u32[]{:S(2)}) copy-start(bf16[1024,1024]{1,0:T(8,128)(2,1)} %param.9) | copy-start | bytes 6291460
  (24 other events, 65.7 us)
Sparse Core Ops, SparseCore 0:
  10.3 63.4 all-gather.1
  393.0 132.7 reduce-scatter.1
where the time goes:
time: 542 us; the launch traced here: 533 us
  matrix products  148 us (27%)
  waiting for transfers between devices  130 us (24%)
  local copies, waits for them, and re-layouts  74.7 us (14%)
  blocking collectives  69.5 us (13%)
  other arithmetic  51.6 us (10%)
  starting transfers between devices  43.9 us (8%)
  between operations  15.2 us (3%)
    reduce_scatter x1, waiting for transfers between devices, local(): lax.psum_scatter(jnp.einsum('tr,tc->rc', block, grad_proj, preferred_elem...  54.8 us
    psum x1, blocking collectives, local(): tap_grads = lax.psum(tap_terms, 'tm')  54.7 us
    all_gather x1, waiting for transfers between devices, local(): lax.all_gather(w_in, 'tm', axis=0, tiled=True)  53.9 us
    dot_general x6, matrix products, signal_of(): blocks = jnp.einsum('ka,ckb->cab', first_both, turned, precision=HIGHEST)  42.6 us
    dot_general x6, matrix products, signal_of(): back = jnp.einsum('ckm,mb->ckb', joined, inverse_second, precision=HIGHEST)  41 us
    dot_general x6, matrix products, spectrum(): jnp.einsum('ckb,bm->ckm', turned, forward_second, precision=HIGHEST)  40.9 us
    unnamed x94, local copies, waits for them, and re-layouts  25.1 us
    all_to_all x4, starting transfers between devices, to_channels(): lax.all_to_all(split_time(series), 'tm', split_axis=1, concat_axis=0, til...  22.3 us
  transfers between devices with their start and end apart: 11, of which 6 were waited for; matrix products, arithmetic and copies ran while one was open for 23% of the time, Pallas kernels for 0%

commit v1 on v0

v1 whole, which is shorter than its diff:
```python
import math

import jax
import jax.numpy as jnp
from jax import lax
from jax.sharding import PartitionSpec as P

DENSE_LIMIT = 4096


def widen(array):
    return array.astype(jnp.float32)


def narrow(array):
    return array.astype(jnp.bfloat16)


def dense_table(total):
    half = total // 2
    inner = 1 << (total.bit_length() - 1) // 2
    outer = half // inner
    step = lax.optimization_barrier(jnp.arange(half, dtype=jnp.int32))
    unit = 2.0 * math.pi / total

    def cis(count, stride):
        index = jnp.arange(count, dtype=jnp.int32)[:, None] * stride * step[None, :] % total
        angle = unit * index.astype(jnp.float32)
        return (jnp.cos(angle), jnp.sin(angle))

    coarse_cos, coarse_sin = cis(outer, inner)
    fine_cos, fine_sin = cis(inner, 1)
    left = jnp.stack([coarse_cos, -coarse_sin])[:, :, None, :]
    right = jnp.stack([-coarse_sin, -coarse_cos])[:, :, None, :]
    table = (left * fine_cos + right * fine_sin).reshape(total, half)
    row = lax.broadcasted_iota(jnp.int32, (total, half), 0)
    parity = (1 - 2 * (step % 2)).astype(jnp.float32)
    return narrow(jnp.where(row == half, parity[None, :], table))


class Dense:
    def __init__(self, total):
        self.half = total // 2
        self.table = dense_table(total)
        first = lax.broadcasted_iota(jnp.int32, (1, self.half), 1) == 0
        self.first = first
        self.scale = jnp.where(first, 1.0 / total, 2.0 / total).astype(jnp.float32)

    def spectrum(self, series):
        both = lax.dot_general(
            series, self.table, (((1,), (1,)), ((), ())), preferred_element_type=jnp.float32
        )
        return (both[:, : self.half], both[:, self.half :])

    def product(self, left, right, conjugate):
        left_re, left_im = left
        right_re, right_im = right
        across = left_im * right_im
        if conjugate:
            real = left_re * right_re + jnp.where(self.first, 0.0, across)
            imag = left_im * right_re - left_re * right_im
        else:
            real = left_re * right_re - jnp.where(self.first, 0.0, across)
            imag = left_re * right_im + left_im * right_re
        imag = jnp.where(self.first, across, imag)
        return (real * self.scale, imag * self.scale)

    def signal(self, pair):
        joined = narrow(jnp.concatenate(pair, axis=1))
        return jnp.dot(joined, self.table, preferred_element_type=jnp.float32)


def cis_tables(count_a, count_b, modulus):
    left = jnp.arange(count_a, dtype=jnp.int32)[:, None]
    right = jnp.arange(count_b, dtype=jnp.int32)[None, :]
    angle = 2.0 * math.pi / modulus * (left * right % modulus).astype(jnp.float32)
    return (jnp.cos(angle), jnp.sin(angle))


class Factored:
    def __init__(self, total):
        bits = total.bit_length() - 1
        first_len = 1 << (bits + 1) // 2
        second_len = total // first_len
        first_cos, first_sin = cis_tables(first_len, first_len // 2, first_len)
        second_cos, second_sin = cis_tables(second_len, second_len, second_len)
        self.total = total
        self.second_len = second_len
        self.twist_cos, self.twist_sin = cis_tables(first_len, second_len, total)
        self.first_both = jnp.concatenate([first_cos, -first_sin], axis=0)
        self.forward = jnp.block([[second_cos, -second_sin], [second_sin, second_cos]])
        self.inverse = jnp.block([[second_cos, second_sin], [-second_sin, second_cos]])

    def spectrum(self, series):
        series = widen(series)
        channels, length = series.shape
        rows_k = self.twist_cos.shape[0]
        half = self.first_both.shape[1]
        blocks = series.reshape(channels, half, length // half)
        part = jnp.einsum("ka,cab->ckb", self.first_both, blocks)
        part_re = part[:, :rows_k]
        part_im = part[:, rows_k:]
        turn_re = part_re * self.twist_cos + part_im * self.twist_sin
        turn_im = part_im * self.twist_cos - part_re * self.twist_sin
        turned = jnp.concatenate([turn_re, turn_im], axis=2)
        result = jnp.einsum("ckb,bm->ckm", turned, self.forward)
        return (result[:, :, : self.second_len], result[:, :, self.second_len :])

    def product(self, left, right, conjugate):
        left_re, left_im = left
        right_re, right_im = right
        if conjugate:
            right_im = -right_im
        return (left_re * right_re - left_im * right_im, left_re * right_im + left_im * right_re)

    def signal(self, pair):
        joined = jnp.concatenate(pair, axis=2)
        back = jnp.einsum("ckm,mb->ckb", joined, self.inverse)
        back_re = back[:, :, : self.second_len]
        back_im = back[:, :, self.second_len :]
        turn_re = back_re * self.twist_cos - back_im * self.twist_sin
        turn_im = back_im * self.twist_cos + back_re * self.twist_sin
        turned = jnp.concatenate([turn_re, turn_im], axis=1)
        blocks = jnp.einsum("ka,ckb->cab", self.first_both, turned)
        return blocks.reshape(joined.shape[0], -1) * (1.0 / self.total)


def delayed(array, steps):
    length = array.shape[1]
    return jnp.pad(array, ((0, 0), (steps, 0)))[:, :length]


def advanced(array, steps):
    return jnp.pad(array, ((0, 0), (0, steps)))[:, steps:]


def local(token_ids, field_offsets, embed_table, w_in, short_taps, filters, cotangent):
    rows, width = cotangent.shape
    fields = token_ids.shape[1]
    peers = lax.axis_size("tm")
    me = lax.axis_index("tm")
    chans = width // peers
    length = rows * peers
    vocab = embed_table.shape[0]

    w_part = w_in.reshape(chans, 3, peers, chans).transpose(2, 0, 1, 3).reshape(peers, chans, 3 * chans)
    cot_part = cotangent.reshape(rows, peers, chans).transpose(1, 2, 0)
    tok_part = narrow(token_ids).T.reshape(1, chans, -1)
    tok_part = jnp.broadcast_to(tok_part, (peers,) + tok_part.shape[1:])
    sent = jnp.concatenate([w_part, cot_part, tok_part], axis=2)
    got = lax.all_to_all(sent, "tm", split_axis=0, concat_axis=0, tiled=True)
    w_own = got[:, :, : 3 * chans].reshape(width, 3 * chans)
    upstream = widen(got[:, :, 3 * chans : 3 * chans + rows].transpose(1, 0, 2).reshape(chans, length))
    tokens = got[:, :, 3 * chans + rows :].reshape(peers, fields, rows)
    tokens = tokens.transpose(1, 0, 2).reshape(fields, length).astype(jnp.int32)
    row_index = tokens + field_offsets[:, None]

    codes = lax.broadcasted_iota(jnp.int32, (vocab, length), 0)
    counts = jnp.zeros((vocab, length), jnp.float32)
    for field in range(fields):
        counts = counts + jnp.where(codes == row_index[field][None, :], 1.0, 0.0)
    embedded = narrow(
        jnp.einsum("vr,vt->rt", embed_table, narrow(counts), preferred_element_type=jnp.float32)
    )
    proj = narrow(jnp.einsum("rc,rt->ct", w_own, embedded, preferred_element_type=jnp.float32))
    taps = lax.dynamic_index_in_dim(short_taps.reshape(3, 3, peers, chans), me, 2, keepdims=False)
    taps = taps.reshape(3, 3 * chans, 1)
    proj_wide = widen(proj)
    lags = (proj_wide, delayed(proj_wide, 1), delayed(proj_wide, 2))
    mixed = narrow(taps[0] * lags[0] + taps[1] * lags[1] + taps[2] * lags[2])
    values = mixed[:chans]
    first_gate = widen(mixed[chans : 2 * chans])
    second_gate = widen(mixed[2 * chans :])

    transform = (Dense if 2 * length <= DENSE_LIMIT else Factored)(2 * length)

    def spectra(*series):
        whole = transform.spectrum(jnp.concatenate(series, axis=0))
        return [
            tuple(part[i * chans : (i + 1) * chans] for part in whole) for i in range(len(series))
        ]

    def signals(*pairs):
        whole = transform.signal(tuple(jnp.concatenate(parts, axis=0) for parts in zip(*pairs)))
        return [whole[i * chans : (i + 1) * chans] for i in range(len(pairs))]

    grad_conv2 = narrow(upstream * second_gate)
    first_spec, second_spec, value_spec, grad_spec2 = spectra(
        filters[0], filters[1], values, grad_conv2
    )
    first_conv, grad_mix = signals(
        transform.product(value_spec, first_spec, False),
        transform.product(grad_spec2, second_spec, True),
    )
    first_conv = widen(narrow(first_conv))
    grad_mix = widen(narrow(grad_mix))
    first_mix = narrow(first_gate * first_conv)
    grad_gate1 = narrow(grad_mix * first_conv)
    grad_conv1 = narrow(grad_mix * first_gate)
    mix_spec, grad_spec1 = spectra(first_mix, grad_conv1)
    second_conv, grad_values, filter_one, filter_two = signals(
        transform.product(mix_spec, second_spec, False),
        transform.product(grad_spec1, first_spec, True),
        transform.product(grad_spec1, value_spec, True),
        transform.product(grad_spec2, mix_spec, True),
    )
    second_conv = widen(narrow(second_conv))
    mixer_out = narrow(second_gate * second_conv)
    grad_gate2 = narrow(upstream * second_conv)
    filter_grads = jnp.stack([filter_one, filter_two], axis=0)
    grad_mixed = jnp.concatenate([narrow(grad_values), grad_gate1, grad_gate2], axis=0)
    grad_wide = widen(grad_mixed)
    grad_proj = narrow(
        taps[0] * grad_wide + taps[1] * advanced(grad_wide, 1) + taps[2] * advanced(grad_wide, 2)
    )
    tap_terms = jnp.stack([jnp.sum(grad_wide * lag, axis=1) for lag in lags], axis=0)
    weight_terms = narrow(
        jnp.einsum("rt,ct->rc", embedded, grad_proj, preferred_element_type=jnp.float32)
    )

    weight_part = weight_terms.reshape(peers, chans, 3 * chans)
    mixer_part = mixer_out.reshape(chans, peers, rows).transpose(1, 0, 2)
    tap_part = narrow(tap_terms).reshape(1, chans, -1)
    tap_part = jnp.broadcast_to(tap_part, (peers,) + tap_part.shape[1:])
    back = lax.all_to_all(
        jnp.concatenate([weight_part, mixer_part, tap_part], axis=2),
        "tm",
        split_axis=0,
        concat_axis=0,
        tiled=True,
    )
    weight_grads = widen(
        back[:, :, : 3 * chans].reshape(peers, chans, 3, chans).transpose(1, 2, 0, 3)
    ).reshape(chans, 3 * width)
    mixer_rows = back[:, :, 3 * chans : 3 * chans + rows].reshape(width, rows).T
    tap_grads = widen(
        back[:, :, 3 * chans + rows :].reshape(peers, 3, 3, chans).transpose(1, 2, 0, 3)
    ).reshape(3, 3 * width)
    return (mixer_rows, weight_grads, tap_grads, filter_grads)


def solution(mesh):
    return jax.shard_map(
        local,
        mesh=mesh,
        in_specs=(
            P(("groups", "tm"), None),
            P("groups"),
            P(),
            P("tm", None),
            P(),
            P(None, "tm", None),
            P(("groups", "tm"), None),
        ),
        out_specs=(
            P(("groups", "tm"), None),
            P(("groups", "tm"), None),
            P("groups", None),
            P("groups", "tm", None),
        ),
        check_vma=False,
    )
```

time: 542 us -> 154 us (0.28); the launches traced: 533 us -> 153 us
  waiting for transfers between devices: 130 us -> 17.9 us
  matrix products: 148 us -> 66.2 us
  blocking collectives: 69.5 us -> 0 us
  local copies, waits for them, and re-layouts: 74.7 us -> 21.9 us
  starting transfers between devices: 43.9 us -> 11.9 us
  other arithmetic: 51.6 us -> 34.3 us
  between operations: 15.2 us -> 1.01 us
    dot_general x26 -> x7, matrix products: 148 us -> 66.2 us  [the longest x2 30.3 us: spectrum(): lax.dot_general(series, self.table, (((1,), (1,)), ((), ())), preferred_e...]
    reduce_scatter x1 -> x0, waiting for transfers between devices: 54.8 us -> none  [local(): lax.psum_scatter(jnp.einsum('tr,tc->rc', block, grad_proj, preferred_elem...]
    psum x1 -> x0, blocking collectives: 54.7 us -> none  [local(): tap_grads = lax.psum(tap_terms, 'tm')]
    all_gather x1 -> x0, waiting for transfers between devices: 53.9 us -> none  [local(): lax.all_gather(w_in, 'tm', axis=0, tiled=True)]
    all_to_all x7 -> x2, starting transfers between devices: 39.6 us -> 11.9 us  [the longest x1 6.61 us: local(): got = lax.all_to_all(sent, 'tm', split_axis=0, concat_axis=0, tiled=True)]
    unnamed x94 -> x26, local copies, waits for them, and re-layouts: 25.1 us -> 3.95 us
    sub x7 -> x0, other arithmetic: 20.7 us -> none  [the longest x4 11.8 us: product(): left_re * right_re - left_im * right_im]
    all_to_all x1 -> x0, blocking collectives: 14.8 us -> none  [to_time(): lax.all_to_all(time_major(block), 'tm', split_axis=0, concat_axis=1, tile...]
  transfers between devices with their start and end apart: 11 -> 2, of which waited for: 6 -> 2; matrix products, arithmetic and copies ran while one was open for 23% -> 14% of each run, Pallas kernels for 0% -> 0%
where the time goes in v1:
time: 154 us; the launch traced here: 153 us
  matrix products  66.2 us (43%)
  other arithmetic  34.3 us (22%)
  local copies, waits for them, and re-layouts  21.9 us (14%)
  waiting for transfers between devices  17.9 us (12%)
  starting transfers between devices  11.9 us (8%)
    dot_general x2, matrix products, spectrum(): lax.dot_general(series, self.table, (((1,), (1,)), ((), ())), preferred_e...  30.3 us
    dot_general x2, matrix products, signal(): return jnp.dot(joined, self.table, preferred_element_type=jnp.float32)  19.8 us
    all_to_all x1, waiting for transfers between devices, local(): lax.all_to_all(jnp.concatenate([weight_part, mixer_part, tap_part], axis=...  17.2 us
    convert_element_type x4, other arithmetic, narrow(): return array.astype(jnp.bfloat16)  11.1 us
    dot_general x1, matrix products, local(): jnp.einsum('vr,vt->rt', embed_table, narrow(counts), preferred_element_ty...  10.9 us
    reshape x3, local copies, waits for them, and re-layouts, local(): weight_grads = widen(back[:, :, :3 * chans].reshape(peers, chans, 3, chan...  7.68 us
    all_to_all x1, starting transfers between devices, local(): got = lax.all_to_all(sent, 'tm', split_axis=0, concat_axis=0, tiled=True)  6.61 us
    add x1, other arithmetic, dense_table(): table = (left * fine_cos + right * fine_sin).reshape(total, half)  6.13 us
  transfers between devices with their start and end apart: 2, of which 2 were waited for; matrix products, arithmetic and copies ran while one was open for 14% of the time, Pallas kernels for 0%

profile of v1, /device:TPU:9, one launch (start us, length us, event | category | flops | bytes accessed | tf_op | source)
XLA Modules:
  0.0 153.2 jit_solution(3301267026880787157)
XLA Ops:
  3.8 1.5 reshape.328
  5.3 1.6 %copy.51 = bf16[64,3,16,64]{0,3,1,2:T(8,128)(2,1)} copy(bf16[64,3,16,64]{3,2,1,0:T(8,128)(2,1)S(1)} %reshape.328) | data formatting | bytes 786432 | tf_op jit(solution)/shard_map/reshape | solution.py:146
  7.0 1.6 %pad_maximum_fusion = bf16[16,64,336]{1,2,0:T(8,128)(2,1)S(1)} fusion(bf16[16,64,16]{1,2,0:T(8,128)(2,1)S(1)} %broadcast_in_dim.136, bf16[16,64,128]{1,2,0:T(8,128)(2,1)} %bitcast.72, bf16[16,64,192]{1,2,0:T(8,128)(2,1)} %bitcast.69), kind=kLoop, calls=%fused_computation.56 | loop fusion | flops 2064384 | bytes 1376256 | tf_op jit(solution)/shard_map/concatenate | solution.py:150
  8.5 1.4 copy.55
  9.9 6.6 %all-to-all-start = ((bf16[16,64,336]{2,1,0:T(8,128)(2,1)}), bf16[16,64,336]{2,1,0:T(8,128)(2,1)S(1)}, u32[]{:S(2)}, u32[]{:S(2)}) async-start(bf16[16,64,336]{2,1,0:T(8,128)(2,1)} %copy.55), calls=%async_computation | async-start | bytes 1572864 | tf_op jit(solution)/shard_map/all_to_all | solution.py:151
  16.5 2.0 %fusion.75 = (f32[64,2048]{1,0:T(8,128)S(1)}, f32[64,2048]{1,0:T(8,128)S(1)}) fusion(s32[2048]{0:T(1024)S(1)} %iota.107), kind=kLoop, calls=%fused_computation.141 | loop fusion | flops 1835008 | bytes 1056768 | tf_op jit(solution)/shard_map/cos | solution.py:29
  19.8 6.1 %multiply_add_fusion = bf16[2,32,64,2048]{3,2,1,0:T(8,128)(2,1)S(1)} fusion(f32[64,2048]{1,0:T(8,128)S(1)} %get-tuple-element.61, f32[2,32,2048]{2,1,0:T(8,128)S(1)} %get-tuple-element.48, f32[64,2048]{1,0:T(8,128)S(1)} %get-tuple-element.60, f32[2,32,2048]{2,1,0:T(8,128)S(1)} %get-tuple-element.47), kind=kLoop, calls=%fused_computation.2 | loop fusion | flops 33554432 | bytes 18874368 | tf_op jit(solution)/shard_map/add | solution.py:35
  26.0 8.1 %fusion = bf16[4096,2048]{1,0:T(8,128)(2,1)} fusion(bf16[2,32,64,2048]{3,2,1,0:T(8,128)(2,1)S(1)} %multiply_add_fusion, bf16[2048]{0:T(1024)(128)(2,1)S(1)} %fusion.81, pred[4096]{0:T(1024)(128)(4,1)S(1)} %iota_compare_fusion.8), kind=kLoop, calls=%fused_computation.1 | loop fusion | flops 8388608 | bytes 33562624 | tf_op jit(solution)/shard_map/convert_element_type | solution.py:16
  36.6 10.9 %fusion.12 = bf16[2048,1024]{1,0:T(8,128)(2,1)S(1)} fusion(bf16[1024,1024]{1,0:T(8,128)(2,1)S(1)} %copy-done, s32[2048]{0:T(1024)S(1)} %bitcast.78, s32[2048]{0:T(1024)S(1)} %bitcast.79, s32[2048]{0:T(1024)S(1)} %bitcast.80, s32[2048]{0:T(1024)S(1)} %bitcast.81, s32[2048]{0:T(1024)S(1)} %bitcast.82, s32[2048]{0:T(1024)S(1)} %bitcast.83, ...), kind=kOutput, calls=%fused_computation.23 | convolution fusion | flops 4347396096 | bytes 6356992 | tf_op jit(solution)/shard_map/vr,vt->rt/dot_general | solution.py:163
  47.5 1.6 %fusion.13 = f32[192,2048]{1,0:T(8,128)S(1)} fusion(bf16[1024,192]{1,0:T(8,128)(2,1)S(1)} %bitcast.71, bf16[2048,1024]{1,0:T(8,128)(2,1)S(1)} %fusion.12), kind=kOutput, calls=%fused_computation.25 | convolution fusion | flops 806092800 | bytes 6160384 | tf_op jit(solution)/shard_map/rc,rt->ct/dot_general | solution.py:165
  51.5 18.8 %fusion.35 = f32[256,4096]{1,0:T(8,128)} fusion(bf16[4096,2048]{1,0:T(8,128)(2,1)} %fusion, bf16[64,2048]{1,0:T(8,128)(2,1)S(1)} %fusion.54, bf16[64,2048]{1,0:T(8,128)(2,1)S(1)} %slice.213, bf16[64,2048]{1,0:T(8,128)(2,1)S(1)} %copy-done.9, bf16[64,2048]{1,0:T(8,128)(2,1)S(1)} %copy-done.8), kind=kOutput, calls=%fused_computation.58 | convolution fusion | flops 4299161600 | bytes 22020096 | tf_op jit(solution)/shard_map/dot_general | solution.py:50
  70.3 2.6 %multiply_convert_fusion.11 = (bf16[64,2048]{1,0:T(8,128)(2,1)S(1)}, bf16[64,2048]{1,0:T(8,128)(2,1)S(1)}, bf16[64,2048]{1,0:T(8,128)(2,1)S(1)}, bf16[64,2048]{1,0:T(8,128)(2,1)S(1)}) fusion(f32[256,4096]{1,0:T(8,128)} %fusion.35, f32[2048]{0:T(1024)S(1)} %broadcast_select_fusion, pred[2048]{0:T(1024)(128)(4,1)S(1)} %iota_compare_fusion.9), kind=kLoop, calls=%fused_computation.118 | loop fusion | flops 3145728 | bytes 5253120 | tf_op jit(solution)/shard_map/convert.35
  72.9 8.1 %convolution_convert_fusion.1 = bf16[128,2048]{1,0:T(8,128)(2,1)S(1)} fusion(bf16[4096,2048]{1,0:T(8,128)(2,1)} %fusion, bf16[64,2048]{1,0:T(8,128)(2,1)S(1)} %get-tuple-element.36, bf16[64,2048]{1,0:T(8,128)(2,1)S(1)} %get-tuple-element.37, bf16[64,2048]{1,0:T(8,128)(2,1)S(1)} %get-tuple-element.35, bf16[64,2048]{1,0:T(8,128)(2,1)S(1)} %get-tuple-element.34), kind=kOutput, calls=%fused_computation.26 | convolution fusion | flops 2151940096 | bytes 18350080 | tf_op jit(solution)/shard_map/dot_general | solution.py:70
  81.0 1.8 %fusion.55 = (bf16[64,2048]{1,0:T(8,128)(2,1)S(1)}, bf16[64,2048]{1,0:T(8,128)(2,1)}, bf16[64,2048]{1,0:T(8,128)(2,1)S(1)}) fusion(bf16[128,2048]{1,0:T(8,128)(2,1)S(1)} %convolution_convert_fusion.1, bf16[192,2048]{1,0:T(8,128)(2,1)} %copy-done.5), kind=kLoop, calls=%fused_computation.89 | loop fusion | flops 1179648 | bytes 1572864 | tf_op jit(solution)/shard_map/convert_element_type | solution.py:16
  82.9 11.5 %fusion.63 = f32[128,4096]{1,0:T(8,128)S(1)} fusion(bf16[4096,2048]{1,0:T(8,128)(2,1)} %fusion, bf16[64,2048]{1,0:T(8,128)(2,1)} %get-tuple-element.41, bf16[64,2048]{1,0:T(8,128)(2,1)S(1)} %get-tuple-element.40), kind=kOutput, calls=%fused_computation.102 | convolution fusion | flops 2148532224 | bytes 19398656 | tf_op jit(solution)/shard_map/dot_general | solution.py:50
  94.4 2.6 %multiply_convert_fusion.7 = (bf16[64,2048]{1,0:T(8,128)(2,1)S(1)}, bf16[64,2048]{1,0:T(8,128)(2,1)S(1)}, bf16[64,2048]{1,0:T(8,128)(2,1)S(1)}, bf16[64,2048]{1,0:T(8,128)(2,1)S(1)}) fusion(f32[128,4096]{1,0:T(8,128)S(1)} %fusion.63, f32[256,4096]{1,0:T(8,128)} %fusion.35, f32[2048]{0:T(1024)S(1)} %broadcast_select_fusion, ...), kind=kLoop, calls=%fused_computation.114 | loop fusion | flops 3407872 | bytes 6301696 | tf_op jit(solution)/shard_map/convert.25
  98.1 11.6 %fusion.91 = (bf16[256,2048]{1,0:T(8,128)(2,1)S(1)}, f32[256,2048]{1,0:T(8,128)}) fusion(bf16[4096,2048]{1,0:T(8,128)(2,1)} %fusion, bf16[64,2048]{1,0:T(8,128)(2,1)S(1)} %get-tuple-element.28, bf16[64,2048]{1,0:T(8,128)(2,1)S(1)} %get-tuple-element.31, bf16[64,2048]{1,0:T(8,128)(2,1)S(1)} %get-tuple-element.29, ...), kind=kOutput, calls=%fused_computation.173 | convolution fusion | flops 4312268800 | bytes 22020096 | tf_op jit(solution)/shard_map/dot_general | solution.py:70
  111.2 1.4 multiply_reduce_fusion.2
  113.1 3.7 %convolution_convert_fusion.2 = bf16[1024,192]{0,1:T(8,128)(2,1)S(1)} fusion(bf16[2048,1024]{1,0:T(8,128)(2,1)} %copy-done.6, f32[192,2048]{1,0:T(8,128)S(1)} %fusion.89, f32[192]{0:T(256)S(1)} %mul.376, f32[192]{0:T(256)S(1)} %mul.373, f32[192]{0:T(256)S(1)} %mul.370), kind=kOutput, calls=%fused_computation.57 | convolution fusion | flops 807862272 | bytes 6162688 | tf_op jit(solution)/shard_map/rt,ct->rc/dot_general | solution.py:218
  118.3 5.3 %all-to-all-start.1 = ((bf16[16,64,329]{2,1,0:T(8,128)(2,1)}), bf16[16,64,329]{2,1,0:T(8,128)(2,1)S(1)}, u32[]{:S(2)}, u32[]{:S(2)}) async-start(bf16[16,64,329]{2,1,0:T(8,128)(2,1)} %pad_maximum_fusion.3), calls=%async_computation.1 | async-start | bytes 1572864 | tf_op jit(solution)/shard_map/all_to_all | solution.py:225
  126.0 17.2 %all-to-all-done.1 = bf16[16,64,329]{2,1,0:T(8,128)(2,1)S(1)} async-done(((bf16[16,64,329]{2,1,0:T(8,128)(2,1)}), bf16[16,64,329]{2,1,0:T(8,128)(2,1)S(1)}, u32[]{:S(2)}, u32[]{:S(2)}) %all-to-all-start.1) | async-done | bytes 673824 | tf_op jit(solution)/shard_map/all_to_all | solution.py:225
  144.3 1.7 %copy.59 = f32[16,64,192]{1,2,0:T(8,128)} copy(f32[16,64,192]{2,1,0:T(8,128)S(1)} %slice_convert_fusion) | data formatting | bytes 1572864 | tf_op jit(solution)/shard_map/reshape | solution.py:234
  145.9 3.3 %copy.60 = f32[64,3,16,64]{3,2,1,0:T(8,128)} copy(f32[64,3,16,64]{0,3,1,2:T(8,128)} %bitcast.68) | data formatting | bytes 1572864 | tf_op jit(solution)/shard_map/reshape | solution.py:234
  149.2 2.7 %reshape.343 = f32[64,3072]{1,0:T(8,128)} reshape(f32[64,3,16,64]{3,2,1,0:T(8,128)} %copy.60) | data formatting | bytes 1572864 | tf_op jit(solution)/shard_map/reshape | solution.py:234
  (75 shorter events, 18.4 us)
Async XLA Ops:
  0.6 35.9 %copy-start = (bf16[1024,1024]{1,0:T(8,128)(2,1)S(1)}, bf16[1024,1024]{1,0:T(8,128)(2,1)}, u32[]{:S(2)}) copy-start(bf16[1024,1024]{1,0:T(8,128)(2,1)} %param.9) | copy-start | bytes 6291460
  9.9 26.2 %all-to-all-start = ((bf16[16,64,336]{2,1,0:T(8,128)(2,1)}), bf16[16,64,336]{2,1,0:T(8,128)(2,1)S(1)}, u32[]{:S(2)}, u32[]{:S(2)}) async-start(bf16[16,64,336]{2,1,0:T(8,128)(2,1)} %copy.55), calls=%async_computation | async-start | bytes 1572864 | tf_op jit(solution)/shard_map/all_to_all | solution.py:151
  26.0 8.2 %copy-start.10 = (f32[3,3072]{1,0:T(4,128)S(1)}, f32[3,3072]{1,0:T(4,128)}, u32[]{:S(2)}) copy-start(f32[3,3072]{1,0:T(4,128)} %param.11) | copy-start | bytes 110596
  26.0 8.5 %copy-start.7 = (bf16[2,64,2048]{2,1,0:T(8,128)(2,1)S(1)}, bf16[2,64,2048]{2,1,0:T(8,128)(2,1)}, u32[]{:S(2)}) copy-start(bf16[2,64,2048]{2,1,0:T(8,128)(2,1)} %param.12) | copy-start | bytes 1572868
  34.1 2.3 %copy-start.11 = (s32[8]{0:T(128)S(1)}, s32[8]{0:T(128)}, u32[]{:S(2)}) copy-start(s32[8]{0:T(128)} %param.8) | copy-start | bytes 100
  47.5 1.9 %copy-start.6 = (bf16[2048,1024]{1,0:T(8,128)(2,1)}, bf16[2048,1024]{1,0:T(8,128)(2,1)S(1)}, u32[]{:S(2)}) copy-start(bf16[2048,1024]{1,0:T(8,128)(2,1)S(1)} %fusion.12) | copy-start | bytes 12582916
  49.4 20.9 %copy-start.3 = (f32[192,2048]{1,0:T(8,128)}, f32[192,2048]{1,0:T(8,128)S(1)}, u32[]{:S(2)}) copy-start(f32[192,2048]{1,0:T(8,128)S(1)} %fusion.13) | copy-start | bytes 4718596
  49.4 2.0 %copy-start.8 = (bf16[64,2048]{1,0:T(8,128)(2,1)S(1)}, bf16[64,2048]{1,0:T(8,128)(2,1)}, u32[]{:S(2)}) copy-start(bf16[64,2048]{1,0:T(8,128)(2,1)} %get-tuple-element.45) | copy-start | bytes 786436
  49.4 2.1 %copy-start.9 = (bf16[64,2048]{1,0:T(8,128)(2,1)S(1)}, bf16[64,2048]{1,0:T(8,128)(2,1)}, u32[]{:S(2)}) copy-start(bf16[64,2048]{1,0:T(8,128)(2,1)} %get-tuple-element.46) | copy-start | bytes 786436
  50.4 0.9 copy-start.5
  94.3 3.1 %copy-start.2 = (f32[256,4096]{1,0:T(8,128)S(1)}, f32[256,4096]{1,0:T(8,128)}, u32[]{:S(2)}) copy-start(f32[256,4096]{1,0:T(8,128)} %fusion.35) | copy-start | bytes 12582916
  109.7 1.5 copy-start.4
  118.3 24.9 %all-to-all-start.1 = ((bf16[16,64,329]{2,1,0:T(8,128)(2,1)}), bf16[16,64,329]{2,1,0:T(8,128)(2,1)S(1)}, u32[]{:S(2)}, u32[]{:S(2)}) async-start(bf16[16,64,329]{2,1,0:T(8,128)(2,1)} %pad_maximum_fusion.3), calls=%async_computation.1 | async-start | bytes 1572864 | tf_op jit(solution)/shard_map/all_to_all | solution.py:225
  145.9 7.3 %copy-start.1 = (bf16[1024,1024]{1,0:T(8,128)(2,1)S(1)}, bf16[1024,1024]{1,0:T(8,128)(2,1)}, u32[]{:S(2)}) copy-start(bf16[1024,1024]{1,0:T(8,128)(2,1)} %param.9) | copy-start | bytes 6291460

commit v2 on v1

--- a/solution.py
+++ b/solution.py
@@ -3,9 +3,14 @@
 import jax
 import jax.numpy as jnp
 from jax import lax
+from jax.experimental import pallas as pl
+from jax.experimental.pallas import tpu as pltpu
 from jax.sharding import PartitionSpec as P
 
 DENSE_LIMIT = 4096
+CODES = 128
+CHUNK = 512
+VMEM = 56 << 20
 
 
 def widen(array):
@@ -32,42 +37,285 @@
     fine_cos, fine_sin = cis(inner, 1)
     left = jnp.stack([coarse_cos, -coarse_sin])[:, :, None, :]
     right = jnp.stack([-coarse_sin, -coarse_cos])[:, :, None, :]
-    table = (left * fine_cos + right * fine_sin).reshape(total, half)
-    row = lax.broadcasted_iota(jnp.int32, (total, half), 0)
-    parity = (1 - 2 * (step % 2)).astype(jnp.float32)
-    return narrow(jnp.where(row == half, parity[None, :], table))
-
-
-class Dense:
-    def __init__(self, total):
-        self.half = total // 2
-        self.table = dense_table(total)
-        first = lax.broadcasted_iota(jnp.int32, (1, self.half), 1) == 0
-        self.first = first
-        self.scale = jnp.where(first, 1.0 / total, 2.0 / total).astype(jnp.float32)
-
-    def spectrum(self, series):
-        both = lax.dot_general(
-            series, self.table, (((1,), (1,)), ((), ())), preferred_element_type=jnp.float32
+    return narrow(left * fine_cos + right * fine_sin).reshape(2, half, half)
+
+
+def spread(rows, columns, start):
+    row = lax.broadcasted_iota(jnp.int32, (rows, columns), 0) + start
+    return 1.0 - 2.0 * (row & 1).astype(jnp.float32)
+
+
+def mixer_kernel(
+    table_hbm, signals, gates, convs, gate_grad, filter_grads, table, spec_re, spec_im, prod_re, prod_im, stage, sems
+):
+    half, pair = gates.shape
+    chans = pair // 2
+    total = 2 * half
+    chunk = min(CHUNK, half)
+    steps = half // chunk
+
+    def copy(part, step):
+        rows = pl.ds(pl.multiple_of(step * chunk, chunk), chunk)
+        return pltpu.make_async_copy(
+            table_hbm.at[part, rows], table.at[part, rows], sems.at[part, step]
         )
-        return (both[:, : self.half], both[:, self.half :])
-
-    def product(self, left, right, conjugate):
-        left_re, left_im = left
-        right_re, right_im = right
-        across = left_im * right_im
-        if conjugate:
-            real = left_re * right_re + jnp.where(self.first, 0.0, across)
-            imag = left_im * right_re - left_re * right_im
-        else:
-            real = left_re * right_re - jnp.where(self.first, 0.0, across)
-            imag = left_re * right_im + left_im * right_re
-        imag = jnp.where(self.first, across, imag)
-        return (real * self.scale, imag * self.scale)
-
-    def signal(self, pair):
-        joined = narrow(jnp.concatenate(pair, axis=1))
-        return jnp.dot(joined, self.table, preferred_element_type=jnp.float32)
+
+    for step in range(steps):
+        copy(0, step).start()
+        copy(1, step).start()
+
+    def window(step):
+        return pl.ds(pl.multiple_of(step * chunk, chunk), chunk)
+
+    def dot(left, right):
+        return jnp.dot(left, right, preferred_element_type=jnp.float32)
+
+    parity = 1 - 2 * (lax.broadcasted_iota(jnp.int32, (16, half), 1) & 1)
+    parity = parity.astype(jnp.float32).astype(jnp.bfloat16)
+    lane = lax.broadcasted_iota(jnp.int32, (1, pair), 1)
+    early = lane < chans
+    sign = jnp.where(early, 1.0, -1.0)
+
+    def scales(step):
+        row = lax.broadcasted_iota(jnp.int32, (chunk, pair), 0) + step * chunk
+        return jnp.where(row == 0, 1.0 / total, 2.0 / total)
+
+    def swap(value):
+        return pltpu.roll(value, chans, 1)
+
+    alternating = dot(parity, signals[...])[:1]
+    ends_filter = alternating[:, :pair]
+    ends_value = alternating[:, pair:]
+
+    def first(step, carry):
+        rows = window(step)
+        copy(0, step).wait()
+        spec_re[rows, :] = dot(table[0, rows, :], signals[...])
+        copy(1, step).wait()
+        spec_im[rows, :] = dot(table[1, rows, :], signals[...])
+        other_re, other_im = spec_re[rows, :pair], spec_im[rows, :pair]
+        real, imag = spec_re[rows, pair:], spec_im[rows, pair:]
+        scale = scales(step)
+        prod_re[rows, :pair] = narrow((real * other_re - sign * imag * other_im) * scale)
+        prod_im[rows, :pair] = narrow((sign * real * other_im + imag * other_re) * scale)
+        return carry
+
+    lax.fori_loop(0, steps, first, 0)
+    ends_first = ends_value * ends_filter * (1.0 / total)
+
+    def second(step, carry):
+        rows = window(step)
+        out = dot(table[0, rows, :], prod_re[:, :pair]) + dot(table[1, rows, :], prod_im[:, :pair])
+        out = out + spread(chunk, pair, step * chunk) * ends_first
+        out = widen(narrow(out))
+        stage[rows, :] = narrow(out * widen(gates[rows, :]))
+        gate_grad[rows, :] = narrow(out * swap(out))
+        return carry
+
+    lax.fori_loop(0, steps, second, 0)
+    ends_mix = dot(parity, stage[...])[:1]
+
+    def third(step, carry):
+        rows = window(step)
+        mixed_re = dot(table[0, rows, :], stage[...])
+        mixed_im = dot(table[1, rows, :], stage[...])
+        filt_re, filt_im = swap(spec_re[rows, :pair]), swap(spec_im[rows, :pair])
+        flip_re, flip_im = swap(spec_re[rows, pair:]), swap(spec_im[rows, pair:])
+        left_re = jnp.where(early, flip_re, mixed_re)
+        left_im = jnp.where(early, flip_im, mixed_im)
+        right_re = jnp.where(early, mixed_re, flip_re)
+        right_im = jnp.where(early, mixed_im, flip_im)
+        scale = scales(step)
+        prod_re[rows, :pair] = narrow((mixed_re * filt_re - sign * mixed_im * filt_im) * scale)
+        prod_im[rows, :pair] = narrow((sign * mixed_re * filt_im + mixed_im * filt_re) * scale)
+        prod_re[rows, pair:] = narrow((left_re * right_re + left_im * right_im) * scale)
+        prod_im[rows, pair:] = narrow((left_im * right_re - left_re * right_im) * scale)
+        return carry
+
+    lax.fori_loop(0, steps, third, 0)
+    ends_conv = ends_mix * swap(jnp.broadcast_to(ends_filter, (8, pair)))[:1] * (1.0 / total)
+    flip = swap(jnp.broadcast_to(ends_value, (8, pair)))[:1]
+    ends_lag = ends_mix * flip * (1.0 / total)
+
+    def fourth(step, carry):
+        rows = window(step)
+        out = dot(table[0, rows, :], prod_re[...]) + dot(table[1, rows, :], prod_im[...])
+        weave = spread(chunk, pair, step * chunk)
+        convs[rows, :] = narrow(out[:, :pair] + weave * ends_conv)
+        lagged = (out[:, pair:] + weave * ends_lag).T
+        filter_grads[1, :, rows] = lagged[:chans]
+        filter_grads[0, :, rows] = lagged[chans:]
+        return carry
+
+    lax.fori_loop(0, steps, fourth, 0)
+
+
+def fused_mixer(table, signals, gates):
+    half, pair = gates.shape
+    chans = pair // 2
+    steps = half // min(CHUNK, half)
+    whole = pl.BlockSpec(memory_space=pltpu.VMEM)
+    wide = pltpu.VMEM((half, 2 * pair), jnp.float32)
+    packed = pltpu.VMEM((half, 2 * pair), jnp.bfloat16)
+    flops = 2 * 2 * half * half * 2 * pair * 4
+    return pl.pallas_call(
+        mixer_kernel,
+        out_shape=(
+            jax.ShapeDtypeStruct((half, pair), jnp.bfloat16),
+            jax.ShapeDtypeStruct((half, pair), jnp.bfloat16),
+            jax.ShapeDtypeStruct((2, chans, half), jnp.float32),
+        ),
+        in_specs=[pl.BlockSpec(memory_space=pl.ANY), whole, whole],
+        out_specs=(whole, whole, whole),
+        scratch_shapes=[
+            pltpu.VMEM((2, half, half), jnp.bfloat16),
+            wide,
+            wide,
+            packed,
+            packed,
+            pltpu.VMEM((half, pair), jnp.bfloat16),
+            pltpu.SemaphoreType.DMA((2, steps)),
+        ],
+        compiler_params=pltpu.CompilerParams(vmem_limit_bytes=VMEM),
+        cost_estimate=pl.CostEstimate(
+            flops=flops, bytes_accessed=4 * half * half, transcendentals=0
+        ),
+        name="mixer",
+    )(table, signals, gates)
+
+
+def pack_kernel(w_ref, cot_ref, tok_ref, out_ref):
+    peers, chans, _ = out_ref.shape
+    rows, width = cot_ref.shape
+    tok = tok_ref[...]
+    for peer in range(peers):
+        own = slice(peer * chans, (peer + 1) * chans)
+        pieces = [w_ref[:, j * width + peer * chans : j * width + (peer + 1) * chans] for j in range(3)]
+        pieces += [cot_ref[:chans, own], cot_ref[chans:, own], tok[:chans], tok[chans:]]
+        out_ref[peer] = jnp.concatenate(pieces, axis=1)
+
+
+def unpack_kernel(got_ref, mixer_ref, weight_ref):
+    peers, chans, _ = got_ref.shape
+    width = peers * chans
+    for peer in range(0, peers, 2):
+        low, high = got_ref[peer], got_ref[peer + 1]
+        for j in range(5):
+            own = slice(j * chans, (j + 1) * chans)
+            both = jnp.concatenate([low[:, own], high[:, own]], axis=1)
+            if j < 3:
+                start = j * width + peer * chans
+                weight_ref[:, start : start + 2 * chans] = widen(both)
+            else:
+                top = (j - 3) * chans
+                mixer_ref[top : top + chans, peer * chans : (peer + 2) * chans] = both
+
+
+def local(token_ids, field_offsets, embed_table, w_in, short_taps, filters, cotangent):
+    chans = cotangent.shape[1] // lax.axis_size("tm")
+    dense = 2 * cotangent.shape[0] * lax.axis_size("tm") <= DENSE_LIMIT
+    plan = fast_local if dense and chans == 64 and cotangent.shape[0] == 2 * chans else wide_local
+    return plan(token_ids, field_offsets, embed_table, w_in, short_taps, filters, cotangent)
+
+
+def later(array, steps):
+    return jnp.pad(array, ((steps, 0), (0, 0)))[: array.shape[0]]
+
+
+def earlier(array, steps):
+    return jnp.pad(array, ((0, steps), (0, 0)))[steps:]
+
+
+def fast_local(token_ids, field_offsets, embed_table, w_in, short_taps, filters, cotangent):
+    rows, width = cotangent.shape
+    fields = token_ids.shape[1]
+    peers = lax.axis_size("tm")
+    me = lax.axis_index("tm")
+    chans = width // peers
+    length = rows * peers
+    lanes = 3 * chans + rows + 2 * fields
+    sent = pl.pallas_call(
+        pack_kernel,
+        out_shape=jax.ShapeDtypeStruct((peers, chans, lanes), jnp.bfloat16),
+        name="pack",
+    )(w_in, cotangent, narrow(token_ids))
+    got = lax.all_to_all(sent, "tm", split_axis=0, concat_axis=0, tiled=True)
+    table = dense_table(2 * length)
+    used = jnp.concatenate(
+        [
+            lax.dynamic_slice_in_dim(embed_table, field_offsets[field], CODES, 0)
+            for field in range(fields)
+        ],
+        axis=0,
+    )
+    filter_rows = filters.transpose(2, 0, 1).reshape(length, 2 * chans)
+
+    def halves(start, count):
+        first = got[:, :, start : start + count]
+        second = got[:, :, start + count : start + 2 * count]
+        return jnp.concatenate([first, second], axis=1).reshape(length, count)
+
+    w_own = got[:, :, : 3 * chans].reshape(width, 3 * chans)
+    upstream = widen(halves(3 * chans, chans))
+    tokens = halves(3 * chans + rows, fields)
+    code = lax.broadcasted_iota(jnp.int32, (1, CODES), 1)
+    code = narrow(code)
+    chosen = jnp.concatenate(
+        [narrow(tokens[:, field : field + 1] == code) for field in range(fields)], axis=1
+    )
+    embedded = narrow(jnp.dot(chosen, used, preferred_element_type=jnp.float32))
+    proj = narrow(jnp.dot(embedded, w_own, preferred_element_type=jnp.float32))
+    taps = lax.dynamic_index_in_dim(short_taps.reshape(3, 3, peers, chans), me, 2, keepdims=False)
+    taps = taps.reshape(3, 1, 3 * chans)
+    proj_wide = widen(proj)
+    lags = (proj_wide, later(proj_wide, 1), later(proj_wide, 2))
+    mixed = narrow(taps[0] * lags[0] + taps[1] * lags[1] + taps[2] * lags[2])
+    values = mixed[:, :chans]
+    first_gate = mixed[:, chans : 2 * chans]
+    second_gate = widen(mixed[:, 2 * chans :])
+    grad_conv2 = narrow(upstream * second_gate)
+    convs, gate_grad, filter_grads = fused_mixer(
+        table,
+        jnp.concatenate([filter_rows, values, grad_conv2], axis=1),
+        jnp.concatenate([first_gate, first_gate], axis=1),
+    )
+    second_conv = widen(convs[:, :chans])
+    mixer_out = narrow(second_gate * second_conv)
+    grad_gate2 = narrow(upstream * second_conv)
+    grad_mixed = jnp.concatenate([convs[:, chans:], gate_grad[:, :chans], grad_gate2], axis=1)
+    grad_wide = widen(grad_mixed)
+    grad_proj = narrow(
+        taps[0] * grad_wide + taps[1] * earlier(grad_wide, 1) + taps[2] * earlier(grad_wide, 2)
+    )
+    tap_terms = jnp.stack([jnp.sum(grad_wide * lag, axis=0) for lag in lags], axis=0)
+    weight_terms = narrow(
+        jnp.einsum("tr,tc->rc", embedded, grad_proj, preferred_element_type=jnp.float32)
+    )
+    mixer_part = mixer_out.reshape(peers, 2, chans, chans)
+    tap_part = narrow(tap_terms).reshape(1, chans, -1)
+    tap_part = jnp.broadcast_to(tap_part, (peers,) + tap_part.shape[1:])
+    back = lax.all_to_all(
+        jnp.concatenate(
+            [weight_terms.reshape(peers, chans, -1), mixer_part[:, 0], mixer_part[:, 1], tap_part],
+            axis=2,
+        ),
+        "tm",
+        split_axis=0,
+        concat_axis=0,
+        tiled=True,
+    )
+    mixer_rows, weight_grads = pl.pallas_call(
+        unpack_kernel,
+        out_shape=(
+            jax.ShapeDtypeStruct((rows, width), jnp.bfloat16),
+            jax.ShapeDtypeStruct((chans, 3 * width), jnp.float32),
+        ),
+        name="unpack",
+    )(back)
+    tap_grads = widen(
+        back[:, :, 3 * chans + rows :].reshape(peers, 3, 3, chans).transpose(1, 2, 0, 3)
+    ).reshape(3, 3 * width)
+    return (mixer_rows, weight_grads, tap_grads, filter_grads)
 
 
 def cis_tables(count_a, count_b, modulus):
@@ -134,7 +382,7 @@
     return jnp.pad(array, ((0, 0), (0, steps)))[:, steps:]
 
 
-def local(token_ids, field_offsets, embed_table, w_in, short_taps, filters, cotangent):
+def wide_local(token_ids, field_offsets, embed_table, w_in, short_taps, filters, cotangent):
     rows, width = cotangent.shape
     fields = token_ids.shape[1]
     peers = lax.axis_size("tm")
@@ -172,7 +420,7 @@
     first_gate = widen(mixed[chans : 2 * chans])
     second_gate = widen(mixed[2 * chans :])
 
-    transform = (Dense if 2 * length <= DENSE_LIMIT else Factored)(2 * length)
+    transform = Factored(2 * length)
 
     def spectra(*series):
         whole = transform.spectrum(jnp.concatenate(series, axis=0))

time: 154 us -> 158 us (1.026)
  matrix products: 66.2 us -> 11.2 us
  Pallas kernels: 0 us -> 35 us
  blocking collectives: 0 us -> 25.7 us
  waiting for transfers between devices: 17.9 us -> 0.01 us
  between operations: 1.01 us -> 15.9 us
  local copies, waits for them, and re-layouts: 21.9 us -> 28.4 us
  starting transfers between devices: 11.9 us -> 6.61 us
    dot_general x7 -> x3, matrix products: 66.2 us -> 11.2 us  [the longest x1 6.47 us: fast_local(): embedded = narrow(jnp.dot(chosen, used, preferred_element_type=jnp.float32))]
    pallas_call x0 -> x3, Pallas kernels: none -> 35 us  [the longest x1 30.4 us: fused_mixer(): pl.pallas_call(mixer_kernel, out_shape=(jax.ShapeDtypeStruct((half, pair)...]
    all_to_all x0 -> x1, blocking collectives: none -> 25.7 us  [fast_local(): lax.all_to_all(jnp.concatenate([weight_terms.reshape(peers, chans, -1), m...]
    all_to_all x2 -> x1, waiting for transfers between devices: 17.9 us -> 0.01 us  [fast_local(): got = lax.all_to_all(sent, 'tm', split_axis=0, concat_axis=0, tiled=True)]
    mul x3 -> x5, local copies, waits for them, and re-layouts: 0.25 us -> 15.9 us  [the longest x2 15.7 us: dense_table(): return narrow(left * fine_cos + right * fine_sin).reshape(2, half, half)]
    convert_element_type x4 -> x6, other arithmetic: 11.1 us -> 21.8 us  [narrow(): return array.astype(jnp.bfloat16)]
    reshape x11 -> x5, local copies, waits for them, and re-layouts: 13.1 us -> 2.52 us  [the longest x1 1.31 us: fast_local(): filter_rows = filters.transpose(2, 0, 1).reshape(length, 2 * chans)]
    another operation x5 -> x1, other arithmetic: 6.86 us -> 0.01 us  [fast_local(): jnp.stack([jnp.sum(grad_wide * lag, axis=0) for lag in lags], axis=0)]
  transfers between devices with their start and end apart: 2 -> 1, of which waited for: 2 -> 0; matrix products, arithmetic and copies ran while one was open for 14% -> 30% of each run, Pallas kernels for 0% -> 0%
where the time goes in v2:
time: 158 us; the launch traced here: 156 us
  Pallas kernels  35 us (22%)
  other arithmetic  33.4 us (21%)
  local copies, waits for them, and re-layouts  28.4 us (18%)
  blocking collectives  25.7 us (16%)
  between operations  15.9 us (10%)
  matrix products  11.2 us (7%)
  starting transfers between devices  6.61 us (4%)
    pallas_call x1, Pallas kernels, fused_mixer(): pl.pallas_call(mixer_kernel, out_shape=(jax.ShapeDtypeStruct((half, pair)...  30.4 us
    all_to_all x1, blocking collectives, fast_local(): lax.all_to_all(jnp.concatenate([weight_terms.reshape(peers, chans, -1), m...  25.7 us
    convert_element_type x6, other arithmetic, narrow(): return array.astype(jnp.bfloat16)  21.8 us
    mul x2, local copies, waits for them, and re-layouts, dense_table(): return narrow(left * fine_cos + right * fine_sin).reshape(2, half, half)  15.7 us
    all_to_all x1, starting transfers between devices, fast_local(): got = lax.all_to_all(sent, 'tm', split_axis=0, concat_axis=0, tiled=True)  6.61 us
    dot_general x1, matrix products, fast_local(): embedded = narrow(jnp.dot(chosen, used, preferred_element_type=jnp.float32))  6.47 us
    unnamed x27, local copies, waits for them, and re-layouts  6.01 us
    dot_general x1, matrix products, fast_local(): jnp.einsum('tr,tc->rc', embedded, grad_proj, preferred_element_type=jnp.f...  3.39 us
  transfers between devices with their start and end apart: 1, of which 0 were waited for; matrix products, arithmetic and copies ran while one was open for 30% of the time, Pallas kernels for 0%

profile of v2, /device:TPU:9, one launch (start us, length us, event | category | flops | bytes accessed | tf_op | source)
XLA Modules:
  0.0 156.1 jit_solution(8262576746995469359)
XLA Ops:
  2.1 2.2 %pack.1 = bf16[16,64,336]{2,1,0:T(8,128)(2,1)} custom-call(bf16[64,3072]{1,0:T(8,128)(2,1)} %w_ref.1, bf16[128,1024]{1,0:T(8,128)(2,1)} %cot_ref.1, bf16[128,8]{1,0:T(8,128)(2,1)} %copy.57.tok_ref), custom_call_target="tpu_custom_call" | custom-call | tf_op jit(solution)/shard_map/pack/pallas_call | solution.py:237
  4.3 6.6 %all-to-all-start = ((bf16[16,64,336]{2,1,0:T(8,128)(2,1)}), bf16[16,64,336]{2,1,0:T(8,128)(2,1)S(1)}, u32[]{:S(2)}, u32[]{:S(2)}) async-start(bf16[16,64,336]{2,1,0:T(8,128)(2,1)} %pack.1), calls=%async_computation | async-start | bytes 1572864 | tf_op jit(solution)/shard_map/all_to_all | solution.py:242
  21.9 2.0 %fusion.25 = (f32[64,2048]{1,0:T(8,128)S(1)}, f32[64,2048]{1,0:T(8,128)S(1)}) fusion(s32[2048]{0:T(1024)S(1)} %iota.41), kind=kLoop, calls=%fused_computation.66 | loop fusion | flops 1835008 | bytes 1056768 | tf_op jit(solution)/shard_map/cos | solution.py:34
  24.0 1.1 fusion.26
  25.1 1.3 copy.61
  31.5 7.8 %mul.221 = f32[32,64,2048]{2,1,0:T(8,128)} broadcast(f32[64,2048]{1,0:T(8,128)S(1)} %get-tuple-element.44), dimensions={1,2} | broadcast | bytes 17301504 | tf_op jit(solution)/shard_map/mul | solution.py:40
  39.3 7.8 %mul.215 = f32[32,64,2048]{2,1,0:T(8,128)} broadcast(f32[64,2048]{1,0:T(8,128)S(1)} %get-tuple-element.43), dimensions={1,2} | broadcast | bytes 17301504 | tf_op jit(solution)/shard_map/mul | solution.py:40
  47.1 18.8 %fusion.1.table_hbm = bf16[2,2048,2048]{2,1,0:T(8,128)(2,1)} fusion(f32[2048,2048]{1,0:T(8,128)} %bitcast.49, f32[2,32,2048]{2,1,0:T(8,128)S(1)} %get-tuple-element.39, f32[2048,2048]{1,0:T(8,128)} %bitcast.50, f32[2,32,2048]{2,1,0:T(8,128)S(1)} %get-tuple-element.38), kind=kLoop, calls=%fused_computation.2 | loop fusion | flops 33554432 | bytes 51380224 | tf_op jit(solution)/shard_map/convert_element_type | solution.py:21
  67.5 0.8 dynamic-slice_dynamic-update-slice_fusion.5
  68.3 0.8 dynamic-slice_dynamic-update-slice_fusion.4
  69.1 0.8 dynamic-slice_dynamic-update-slice_fusion.3
  69.9 0.8 dynamic-slice_dynamic-update-slice_fusion.2
  70.7 0.8 dynamic-slice_dynamic-update-slice_fusion.1
  71.4 0.8 dynamic-slice_dynamic-update-slice_fusion
  76.5 6.5 %convolution_convert_fusion = bf16[2048,1024]{1,0:T(8,128)(2,1)S(1)} fusion(pred[2048,1024]{1,0:T(8,128)(4,1)S(1)} %compare_dynamic-update-slice_fusion, bf16[1024,1024]{1,0:T(8,128)(2,1)} %dynamic-slice_dynamic-update-slice_fusion), kind=kOutput, calls=%fused_computation.4 | convolution fusion | flops 4297064448 | bytes 8388608 | tf_op jit(solution)/shard_map/dot_general | solution.py:266
  83.1 1.3 fusion.2
  86.3 1.1 pad_maximum_fusion.6.gates
  87.4 1.3 pad_maximum_fusion.signals
  88.7 30.4 %mixer.1 = (bf16[2048,128]{1,0:T(8,128)(2,1)}, bf16[2048,128]{1,0:T(8,128)(2,1)}, f32[2,64,2048]{2,1,0:T(8,128)}) custom-call(bf16[2,2048,2048]{2,1,0:T(8,128)(2,1)} %fusion.1.table_hbm, bf16[2048,256]{1,0:T(8,128)(2,1)} %pad_maximum_fusion.signals, bf16[2048,128]{1,0:T(8,128)(2,1)} %pad_maximum_fusion.6.gates), custom_call_target="tpu_custom_call" | custom-call | flops 17179869184 | bytes 16777216 | tf_op jit(solution)/shard_map/mixer/pallas_call | solution.py:161
  119.2 1.4 fusion.8
  120.8 1.3 multiply_reduce_fusion.2
  122.7 3.4 %convolution_convert_fusion.2 = bf16[1024,192]{0,1:T(8,128)(2,1)S(1)} fusion(bf16[2048,1024]{1,0:T(8,128)(2,1)} %copy-done.9, f32[2048,192]{1,0:T(8,128)S(1)} %fusion.32, f32[192]{0:T(256)} %copy-done.6, f32[192]{0:T(256)} %copy-done.7, f32[192]{0:T(256)} %copy-done.8), kind=kOutput, calls=%fused_computation.23 | convolution fusion | flops 807862272 | bytes 6162688 | tf_op jit(solution)/shard_map/tr,tc->rc/dot_general | solution.py:292
  126.8 25.7 %all_to_all.10.got_ref = bf16[16,64,329]{2,1,0:T(8,128)(2,1)S(1)} all-to-all(bf16[16,64,329]{2,1,0:T(8,128)(2,1)S(1)} %pad_maximum_fusion.2), channel_id=1, replica_groups=mesh['groups'=2,'tm'=16] {'tm'}, dimensions={0} | all-to-all | bytes 1347584 | tf_op jit(solution)/shard_map/all_to_all | solution.py:297
  153.8 2.3 %unpack.1 = (bf16[128,1024]{1,0:T(8,128)(2,1)}, f32[64,3072]{1,0:T(8,128)}) custom-call(bf16[16,64,329]{2,1,0:T(8,128)(2,1)} %copy-done), custom_call_target="tpu_custom_call" | custom-call | tf_op jit(solution)/shard_map/unpack/pallas_call | solution.py:307
  (69 shorter events, 13.1 us)
Async XLA Ops:
  0.6 10.3 %copy-start.5 = (s32[8]{0:T(128)S(1)}, s32[8]{0:T(128)}, u32[]{:S(2)}) copy-start(s32[8]{0:T(128)} %param.8) | copy-start | bytes 100
  0.6 20.9 %copy-start.4 = (f32[3,3072]{1,0:T(4,128)S(1)}, f32[3,3072]{1,0:T(4,128)}, u32[]{:S(2)}) copy-start(f32[3,3072]{1,0:T(4,128)} %param.11) | copy-start | bytes 110596
  4.3 67.9 %all-to-all-start = ((bf16[16,64,336]{2,1,0:T(8,128)(2,1)}), bf16[16,64,336]{2,1,0:T(8,128)(2,1)S(1)}, u32[]{:S(2)}, u32[]{:S(2)}) async-start(bf16[16,64,336]{2,1,0:T(8,128)(2,1)} %pack.1), calls=%async_computation | async-start | bytes 1572864 | tf_op jit(solution)/shard_map/all_to_all | solution.py:242
  21.7 62.6 %copy-start.6 = (f32[192]{0:T(256)}, f32[192]{0:T(256)S(1)}, u32[]{:S(2)}) copy-start(f32[192]{0:T(256)S(1)} %mul.229) | copy-start | bytes 2308
  21.8 62.6 %copy-start.7 = (f32[192]{0:T(256)}, f32[192]{0:T(256)S(1)}, u32[]{:S(2)}) copy-start(f32[192]{0:T(256)S(1)} %mul.226) | copy-start | bytes 2308
  21.9 62.5 %copy-start.8 = (f32[192]{0:T(256)}, f32[192]{0:T(256)S(1)}, u32[]{:S(2)}) copy-start(f32[192]{0:T(256)S(1)} %mul.199) | copy-start | bytes 2308
  47.1 18.9 %copy-start.1 = (bf16[1024,1024]{1,0:T(8,128)(2,1)S(1)}, bf16[1024,1024]{1,0:T(8,128)(2,1)}, u32[]{:S(2)}) copy-start(bf16[1024,1024]{1,0:T(8,128)(2,1)} %param.9) | copy-start | bytes 6291460
  83.0 1.9 %copy-start.9 = (bf16[2048,1024]{1,0:T(8,128)(2,1)}, bf16[2048,1024]{1,0:T(8,128)(2,1)S(1)}, u32[]{:S(2)}) copy-start(bf16[2048,1024]{1,0:T(8,128)(2,1)S(1)} %convolution_convert_fusion) | copy-start | bytes 12582916
  119.1 1.4 copy-start.2
  119.1 1.6 %copy-start.3 = (bf16[2048,128]{1,0:T(8,128)(2,1)S(1)}, bf16[2048,128]{1,0:T(8,128)(2,1)}, u32[]{:S(2)}) copy-start(bf16[2048,128]{1,0:T(8,128)(2,1)} %get-tuple-element.10) | copy-start | bytes 1572868
  152.5 1.3 copy-start

commit v3 on v2

--- a/solution.py
+++ b/solution.py
@@ -35,9 +35,65 @@
 
     coarse_cos, coarse_sin = cis(outer, inner)
     fine_cos, fine_sin = cis(inner, 1)
-    left = jnp.stack([coarse_cos, -coarse_sin])[:, :, None, :]
-    right = jnp.stack([-coarse_sin, -coarse_cos])[:, :, None, :]
-    return narrow(left * fine_cos + right * fine_sin).reshape(2, half, half)
+    whole = pl.BlockSpec(memory_space=pltpu.VMEM)
+    return pl.pallas_call(
+        table_kernel,
+        grid=(outer,),
+        out_shape=jax.ShapeDtypeStruct((2, half, half), jnp.bfloat16),
+        in_specs=[whole] * 4,
+        out_specs=pl.BlockSpec((2, inner, half), lambda i: (0, i, 0)),
+        cost_estimate=pl.CostEstimate(
+            flops=6 * half * half, bytes_accessed=4 * half * half, transcendentals=0
+        ),
+        compiler_params=pltpu.CompilerParams(vmem_limit_bytes=24 << 20),
+        name="table",
+    )(coarse_cos, coarse_sin, fine_cos, fine_sin)
+
+
+def table_kernel(coarse_cos, coarse_sin, fine_cos, fine_sin, out):
+    row = pl.ds(pl.program_id(0), 1)
+    high_cos, high_sin = coarse_cos[row, :], coarse_sin[row, :]
+    low_cos, low_sin = fine_cos[...], fine_sin[...]
+    out[0] = narrow(high_cos * low_cos - high_sin * low_sin)
+    out[1] = narrow(-(high_sin * low_cos + high_cos * low_sin))
+
+
+def embed_kernel(tokens, used, w_own, embedded, proj):
+    picked = tokens[...]
+    code = lax.broadcasted_iota(jnp.int32, (picked.shape[0], CODES), 1)
+    chosen = [
+        narrow(jnp.where(picked[:, field : field + 1] == code, 1.0, 0.0))
+        for field in range(picked.shape[1])
+    ]
+    rows = narrow(
+        jnp.dot(
+            jnp.concatenate(chosen, axis=1), used[...], preferred_element_type=jnp.float32
+        )
+    )
+    embedded[...] = rows
+    proj[...] = narrow(jnp.dot(rows, w_own[...], preferred_element_type=jnp.float32))
+
+
+def embed(tokens, used, w_own):
+    length, fields = tokens.shape
+    width, columns = w_own.shape
+    block = 256
+    whole = pl.BlockSpec(memory_space=pltpu.VMEM)
+    return pl.pallas_call(
+        embed_kernel,
+        grid=(length // block,),
+        out_shape=(
+            jax.ShapeDtypeStruct((length, width), jnp.bfloat16),
+            jax.ShapeDtypeStruct((length, columns), jnp.bfloat16),
+        ),
+        in_specs=[pl.BlockSpec((block, fields), lambda i: (i, 0)), whole, whole],
+        out_specs=(
+            pl.BlockSpec((block, width), lambda i: (i, 0)),
+            pl.BlockSpec((block, columns), lambda i: (i, 0)),
+        ),
+        compiler_params=pltpu.CompilerParams(vmem_limit_bytes=24 << 20),
+        name="embed",
+    )(tokens, used, w_own)
 
 
 def spread(rows, columns, start):
@@ -45,17 +101,32 @@
     return 1.0 - 2.0 * (row & 1).astype(jnp.float32)
 
 
+def dot(left, right):
+    return jnp.dot(left, right, preferred_element_type=jnp.float32)
+
+
+def quarter(rows, columns, start):
+    turn = (lax.broadcasted_iota(jnp.int32, (rows, columns), 0) + start) & 3
+    real = jnp.where(turn == 0, 1.0, jnp.where(turn == 2, -1.0, 0.0))
+    imag = jnp.where(turn == 1, 1.0, jnp.where(turn == 3, -1.0, 0.0))
+    return (real, imag)
+
+
 def mixer_kernel(
-    table_hbm, signals, gates, convs, gate_grad, filter_grads, table, spec_re, spec_im, prod_re, prod_im, stage, sems
+    table_hbm, signals, gates, convs, gate_grad, lag_re, lag_im, ends, table, spec_re, spec_im, prod_re, prod_im, stage, sems
 ):
     half, pair = gates.shape
+    middle = half // 2
     chans = pair // 2
     total = 2 * half
-    chunk = min(CHUNK, half)
+    chunk = min(CHUNK, middle)
     steps = half // chunk
 
+    def window(step, base=0):
+        return pl.ds(pl.multiple_of(step * chunk + base, chunk), chunk)
+
     def copy(part, step):
-        rows = pl.ds(pl.multiple_of(step * chunk, chunk), chunk)
+        rows = window(step)
         return pltpu.make_async_copy(
             table_hbm.at[part, rows], table.at[part, rows], sems.at[part, step]
         )
@@ -64,26 +135,26 @@
         copy(0, step).start()
         copy(1, step).start()
 
-    def window(step):
-        return pl.ds(pl.multiple_of(step * chunk, chunk), chunk)
-
-    def dot(left, right):
-        return jnp.dot(left, right, preferred_element_type=jnp.float32)
-
     parity = 1 - 2 * (lax.broadcasted_iota(jnp.int32, (16, half), 1) & 1)
     parity = parity.astype(jnp.float32).astype(jnp.bfloat16)
-    lane = lax.broadcasted_iota(jnp.int32, (1, pair), 1)
-    early = lane < chans
+    early = lax.broadcasted_iota(jnp.int32, (1, pair), 1) < chans
     sign = jnp.where(early, 1.0, -1.0)
-
-    def scales(step):
-        row = lax.broadcasted_iota(jnp.int32, (chunk, pair), 0) + step * chunk
-        return jnp.where(row == 0, 1.0 / total, 2.0 / total)
 
     def swap(value):
         return pltpu.roll(value, chans, 1)
 
-    alternating = dot(parity, signals[...])[:1]
+    def keep(step, real, imag, to_re, to_im):
+        rows = window(step)
+        row = lax.broadcasted_iota(jnp.int32, (chunk, pair), 0) + step * chunk
+        scale = jnp.where(row == 0, 1.0 / total, 2.0 / total)
+        real, imag = real * scale, imag * scale
+        cos, sin = quarter(chunk, pair, step * chunk)
+        to_re[rows, :pair] = narrow(real)
+        to_im[rows, :pair] = narrow(imag)
+        to_re[rows, pair:] = narrow(cos * real - sin * imag)
+        to_im[rows, pair:] = narrow(sin * real + cos * imag)
+
+    alternating = dot(parity, signals[...])[:8]
     ends_filter = alternating[:, :pair]
     ends_value = alternating[:, pair:]
 
@@ -95,93 +166,170 @@
         spec_im[rows, :] = dot(table[1, rows, :], signals[...])
         other_re, other_im = spec_re[rows, :pair], spec_im[rows, :pair]
         real, imag = spec_re[rows, pair:], spec_im[rows, pair:]
-        scale = scales(step)
-        prod_re[rows, :pair] = narrow((real * other_re - sign * imag * other_im) * scale)
-        prod_im[rows, :pair] = narrow((sign * real * other_im + imag * other_re) * scale)
+        keep(
+            step,
+            real * other_re - sign * imag * other_im,
+            sign * real * other_im + imag * other_re,
+            prod_re,
+            prod_im,
+        )
         return carry
 
     lax.fori_loop(0, steps, first, 0)
-    ends_first = ends_value * ends_filter * (1.0 / total)
+    ends_first = (ends_value * ends_filter * (1.0 / total))[:1]
 
     def second(step, carry):
         rows = window(step)
-        out = dot(table[0, rows, :], prod_re[:, :pair]) + dot(table[1, rows, :], prod_im[:, :pair])
-        out = out + spread(chunk, pair, step * chunk) * ends_first
-        out = widen(narrow(out))
-        stage[rows, :] = narrow(out * widen(gates[rows, :]))
-        gate_grad[rows, :] = narrow(out * swap(out))
+        both = dot(table[0, rows, :], prod_re[...]) + dot(table[1, rows, :], prod_im[...])
+        weave = spread(chunk, pair, step * chunk) * ends_first
+        for part in range(2):
+            lanes = slice(part * pair, (part + 1) * pair)
+            place = window(step, part * middle)
+            out = widen(narrow(both[:, lanes] + weave))
+            stage[rows, lanes] = narrow(out * widen(gates[place, :]))
+            gate_grad[place, :] = narrow(out * swap(out))
         return carry
 
-    lax.fori_loop(0, steps, second, 0)
-    ends_mix = dot(parity, stage[...])[:1]
+    lax.fori_loop(0, steps // 2, second, 0)
+    ends_both = dot(parity[:, :middle], stage[...])[:8]
+    ends_mix = ends_both[:, :pair] + ends_both[:, pair:]
 
     def third(step, carry):
         rows = window(step)
-        mixed_re = dot(table[0, rows, :], stage[...])
-        mixed_im = dot(table[1, rows, :], stage[...])
+        half_re = dot(table[0, rows, :middle], stage[...])
+        half_im = dot(table[1, rows, :middle], stage[...])
+        cos, sin = quarter(chunk, pair, step * chunk)
+        mixed_re = half_re[:, :pair] + cos * half_re[:, pair:] + sin * half_im[:, pair:]
+        mixed_im = half_im[:, :pair] + cos * half_im[:, pair:] - sin * half_re[:, pair:]
         filt_re, filt_im = swap(spec_re[rows, :pair]), swap(spec_im[rows, :pair])
         flip_re, flip_im = swap(spec_re[rows, pair:]), swap(spec_im[rows, pair:])
         left_re = jnp.where(early, flip_re, mixed_re)
         left_im = jnp.where(early, flip_im, mixed_im)
         right_re = jnp.where(early, mixed_re, flip_re)
         right_im = jnp.where(early, mixed_im, flip_im)
-        scale = scales(step)
-        prod_re[rows, :pair] = narrow((mixed_re * filt_re - sign * mixed_im * filt_im) * scale)
-        prod_im[rows, :pair] = narrow((sign * mixed_re * filt_im + mixed_im * filt_re) * scale)
-        prod_re[rows, pair:] = narrow((left_re * right_re + left_im * right_im) * scale)
-        prod_im[rows, pair:] = narrow((left_im * right_re - left_re * right_im) * scale)
+        keep(
+            step,
+            mixed_re * filt_re - sign * mixed_im * filt_im,
+            sign * mixed_re * filt_im + mixed_im * filt_re,
+            prod_re,
+            prod_im,
+        )
+        keep(
+            step,
+            left_re * right_re + left_im * right_im,
+            left_im * right_re - left_re * right_im,
+            lag_re,
+            lag_im,
+        )
         return carry
 
     lax.fori_loop(0, steps, third, 0)
-    ends_conv = ends_mix * swap(jnp.broadcast_to(ends_filter, (8, pair)))[:1] * (1.0 / total)
-    flip = swap(jnp.broadcast_to(ends_value, (8, pair)))[:1]
-    ends_lag = ends_mix * flip * (1.0 / total)
+    ends_conv = (ends_mix * swap(ends_filter) * (1.0 / total))[:1]
+    ends[...] = ends_mix * swap(ends_value) * (1.0 / total)
 
     def fourth(step, carry):
         rows = window(step)
-        out = dot(table[0, rows, :], prod_re[...]) + dot(table[1, rows, :], prod_im[...])
-        weave = spread(chunk, pair, step * chunk)
-        convs[rows, :] = narrow(out[:, :pair] + weave * ends_conv)
-        lagged = (out[:, pair:] + weave * ends_lag).T
-        filter_grads[1, :, rows] = lagged[:chans]
-        filter_grads[0, :, rows] = lagged[chans:]
+        both = dot(table[0, rows, :], prod_re[...]) + dot(table[1, rows, :], prod_im[...])
+        weave = spread(chunk, pair, step * chunk) * ends_conv
+        convs[rows, :] = narrow(both[:, :pair] + weave)
+        convs[window(step, middle), :] = narrow(both[:, pair:] + weave)
         return carry
 
-    lax.fori_loop(0, steps, fourth, 0)
+    lax.fori_loop(0, steps // 2, fourth, 0)
+
+
+def lag_kernel(table_hbm, lag_re, lag_im, ends, filter_grads, table, sems):
+    half, pair = lag_re.shape[0], lag_re.shape[1] // 2
+    middle = half // 2
+    chans = pair // 2
+    chunk = min(CHUNK, middle)
+    steps = middle // chunk
+
+    def window(step, base=0):
+        return pl.ds(pl.multiple_of(step * chunk + base, chunk), chunk)
+
+    def copy(part, step):
+        rows = window(step)
+        return pltpu.make_async_copy(
+            table_hbm.at[part, rows], table.at[part, rows], sems.at[part, step]
+        )
+
+    for step in range(steps):
+        copy(0, step).start()
+        copy(1, step).start()
+
+    def body(step, carry):
+        rows = window(step)
+        copy(0, step).wait()
+        copy(1, step).wait()
+        both = dot(table[0, rows, :], lag_re[...]) + dot(table[1, rows, :], lag_im[...])
+        weave = spread(chunk, pair, step * chunk) * ends[:1, :]
+        for part in range(2):
+            lagged = (both[:, part * pair : (part + 1) * pair] + weave).T
+            place = window(step, part * middle)
+            filter_grads[1, :, place] = lagged[:chans]
+            filter_grads[0, :, place] = lagged[chans:]
+        return carry
+
+    lax.fori_loop(0, steps, body, 0)
 
 
 def fused_mixer(table, signals, gates):
     half, pair = gates.shape
-    chans = pair // 2
-    steps = half // min(CHUNK, half)
+    steps = half // min(CHUNK, half // 2)
     whole = pl.BlockSpec(memory_space=pltpu.VMEM)
     wide = pltpu.VMEM((half, 2 * pair), jnp.float32)
     packed = pltpu.VMEM((half, 2 * pair), jnp.bfloat16)
-    flops = 2 * 2 * half * half * 2 * pair * 4
+    narrow_out = jax.ShapeDtypeStruct((half, pair), jnp.bfloat16)
+    wide_out = jax.ShapeDtypeStruct((half, 2 * pair), jnp.bfloat16)
     return pl.pallas_call(
         mixer_kernel,
         out_shape=(
-            jax.ShapeDtypeStruct((half, pair), jnp.bfloat16),
-            jax.ShapeDtypeStruct((half, pair), jnp.bfloat16),
-            jax.ShapeDtypeStruct((2, chans, half), jnp.float32),
+            narrow_out,
+            narrow_out,
+            wide_out,
+            wide_out,
+            jax.ShapeDtypeStruct((8, pair), jnp.float32),
         ),
         in_specs=[pl.BlockSpec(memory_space=pl.ANY), whole, whole],
-        out_specs=(whole, whole, whole),
+        out_specs=(whole,) * 5,
         scratch_shapes=[
             pltpu.VMEM((2, half, half), jnp.bfloat16),
             wide,
             wide,
             packed,
             packed,
-            pltpu.VMEM((half, pair), jnp.bfloat16),
+            pltpu.VMEM((half // 2, 2 * pair), jnp.bfloat16),
             pltpu.SemaphoreType.DMA((2, steps)),
         ],
         compiler_params=pltpu.CompilerParams(vmem_limit_bytes=VMEM),
         cost_estimate=pl.CostEstimate(
-            flops=flops, bytes_accessed=4 * half * half, transcendentals=0
+            flops=20 * half * half * pair, bytes_accessed=4 * half * half, transcendentals=0
         ),
         name="mixer",
     )(table, signals, gates)
+
+
+def lag_grads(table, lag_re, lag_im, ends):
+    half, pair = lag_re.shape[0], lag_re.shape[1] // 2
+    middle = half // 2
+    steps = middle // min(CHUNK, middle)
+    whole = pl.BlockSpec(memory_space=pltpu.VMEM)
+    return pl.pallas_call(
+        lag_kernel,
+        out_shape=jax.ShapeDtypeStruct((2, pair // 2, half), jnp.float32),
+        in_specs=[pl.BlockSpec(memory_space=pl.ANY), whole, whole, whole],
+        out_specs=whole,
+        scratch_shapes=[
+            pltpu.VMEM((2, middle, half), jnp.bfloat16),
+            pltpu.SemaphoreType.DMA((2, steps)),
+        ],
+        compiler_params=pltpu.CompilerParams(vmem_limit_bytes=24 << 20),
+        cost_estimate=pl.CostEstimate(
+            flops=4 * half * half * pair, bytes_accessed=3 * half * half, transcendentals=0
+        ),
+        name="lags",
+    )(table, lag_re, lag_im, ends)
 
 
 def pack_kernel(w_ref, cot_ref, tok_ref, out_ref):
@@ -257,14 +405,8 @@
 
     w_own = got[:, :, : 3 * chans].reshape(width, 3 * chans)
     upstream = widen(halves(3 * chans, chans))
-    tokens = halves(3 * chans + rows, fields)
-    code = lax.broadcasted_iota(jnp.int32, (1, CODES), 1)
-    code = narrow(code)
-    chosen = jnp.concatenate(
-        [narrow(tokens[:, field : field + 1] == code) for field in range(fields)], axis=1
-    )
-    embedded = narrow(jnp.dot(chosen, used, preferred_element_type=jnp.float32))
-    proj = narrow(jnp.dot(embedded, w_own, preferred_element_type=jnp.float32))
+    tokens = halves(3 * chans + rows, fields).astype(jnp.int32)
+    embedded, proj = embed(tokens, used, w_own)
     taps = lax.dynamic_index_in_dim(short_taps.reshape(3, 3, peers, chans), me, 2, keepdims=False)
     taps = taps.reshape(3, 1, 3 * chans)
     proj_wide = widen(proj)
@@ -274,7 +416,7 @@
     first_gate = mixed[:, chans : 2 * chans]
     second_gate = widen(mixed[:, 2 * chans :])
     grad_conv2 = narrow(upstream * second_gate)
-    convs, gate_grad, filter_grads = fused_mixer(
+    convs, gate_grad, lag_re, lag_im, ends = fused_mixer(
         table,
         jnp.concatenate([filter_rows, values, grad_conv2], axis=1),
         jnp.concatenate([first_gate, first_gate], axis=1),
@@ -304,6 +446,7 @@
         concat_axis=0,
         tiled=True,
     )
+    filter_grads = lag_grads(table, lag_re, lag_im, ends)
     mixer_rows, weight_grads = pl.pallas_call(
         unpack_kernel,
         out_shape=(

time: 158 us -> 126 us (0.80)
  blocking collectives: 25.7 us -> 0 us
  other arithmetic: 33.4 us -> 12.1 us
  Pallas kernels: 35 us -> 48 us
  waiting for transfers between devices: 0.01 us -> 9.48 us
  matrix products: 11.2 us -> 3.37 us
  starting transfers between devices: 6.61 us -> 12.6 us
  local copies, waits for them, and re-layouts: 28.4 us -> 22.9 us
    all_to_all x1 -> x0, blocking collectives: 25.7 us -> none  [fast_local(): lax.all_to_all(jnp.concatenate([weight_terms.reshape(peers, chans, -1), m...]
    convert_element_type x6 -> x4, other arithmetic: 21.8 us -> 2.98 us  [narrow(): return array.astype(jnp.bfloat16)]
    mul x2 -> x0, local copies, waits for them, and re-layouts: 15.7 us -> none  [dense_table(): return narrow(left * fine_cos + right * fine_sin).reshape(2, half, half)]
    pallas_call x1 -> x4, Pallas kernels: 30.4 us -> 43.5 us  [the longest x1 24 us: fused_mixer(): pl.pallas_call(mixer_kernel, out_shape=(narrow_out, narrow_out, wide_out,...]
    all_to_all x0 -> x1, waiting for transfers between devices: none -> 9.47 us  [fast_local(): lax.all_to_all(jnp.concatenate([weight_terms.reshape(peers, chans, -1), m...]
    unnamed x27 -> x39, local copies, waits for them, and re-layouts: 6.01 us -> 14.6 us
    dot_general x2 -> x0, matrix products: 7.78 us -> none  [the longest x1 6.47 us: fast_local(): embedded = narrow(jnp.dot(chosen, used, preferred_element_type=jnp.float32))]
    all_to_all x0 -> x1, starting transfers between devices: none -> 6.02 us  [fast_local(): lax.all_to_all(jnp.concatenate([weight_terms.reshape(peers, chans, -1), m...]
  transfers between devices with their start and end apart: 1 -> 2, of which waited for: 0 -> 1; matrix products, arithmetic and copies ran while one was open for 30% -> 5% of each run, Pallas kernels for 0% -> 8%
where the time goes in v3:
time: 126 us; the launch traced here: 125 us
  Pallas kernels  48 us (38%)
  local copies, waits for them, and re-layouts  22.9 us (18%)
  between operations  16.2 us (13%)
  starting transfers between devices  12.6 us (10%)
  other arithmetic  12.1 us (10%)
  waiting for transfers between devices  9.48 us (8%)
  matrix products  3.37 us (3%)
    pallas_call x1, Pallas kernels, fused_mixer(): pl.pallas_call(mixer_kernel, out_shape=(narrow_out, narrow_out, wide_out,...  24 us
    unnamed x39, local copies, waits for them, and re-layouts  14.6 us
    all_to_all x1, waiting for transfers between devices, fast_local(): lax.all_to_all(jnp.concatenate([weight_terms.reshape(peers, chans, -1), m...  9.47 us
    pallas_call x1, Pallas kernels, embed(): pl.pallas_call(embed_kernel, grid=(length // block,), out_shape=(jax.Shap...  9.22 us
    all_to_all x1, starting transfers between devices, fast_local(): got = lax.all_to_all(sent, 'tm', split_axis=0, concat_axis=0, tiled=True)  6.61 us
    all_to_all x1, starting transfers between devices, fast_local(): lax.all_to_all(jnp.concatenate([weight_terms.reshape(peers, chans, -1), m...  6.02 us
    pallas_call x1, Pallas kernels, dense_table(): pl.pallas_call(table_kernel, grid=(outer,), out_shape=jax.ShapeDtypeStruc...  5.91 us
    pallas_call x1, Pallas kernels, lag_grads(): pl.pallas_call(lag_kernel, out_shape=jax.ShapeDtypeStruct((2, pair // 2,...  4.28 us
  transfers between devices with their start and end apart: 2, of which 1 were waited for; matrix products, arithmetic and copies ran while one was open for 5% of the time, Pallas kernels for 8%

profile of v3, /device:TPU:9, one launch (start us, length us, event | category | flops | bytes accessed | tf_op | source)
XLA Modules:
  0.0 124.7 jit_solution(6463057207795328798)
XLA Ops:
  2.1 2.2 %pack.1 = bf16[16,64,336]{2,1,0:T(8,128)(2,1)} custom-call(bf16[64,3072]{1,0:T(8,128)(2,1)} %w_ref.1, bf16[128,1024]{1,0:T(8,128)(2,1)} %cot_ref.1, bf16[128,8]{1,0:T(8,128)(2,1)} %copy.38.tok_ref), custom_call_target="tpu_custom_call" | custom-call | tf_op jit(solution)/shard_map/pack/pallas_call | solution.py:385
  4.4 6.6 %all-to-all-start = ((bf16[16,64,336]{2,1,0:T(8,128)(2,1)}), bf16[16,64,336]{2,1,0:T(8,128)(2,1)S(1)}, u32[]{:S(2)}, u32[]{:S(2)}) async-start(bf16[16,64,336]{2,1,0:T(8,128)(2,1)} %pack.1), calls=%async_computation | async-start | bytes 1572864 | tf_op jit(solution)/shard_map/all_to_all | solution.py:390
  22.1 1.0 copy.42
  23.1 2.0 %fusion.21 = (f32[64,2048]{1,0:T(8,128)S(1)}, f32[64,2048]{1,0:T(8,128)S(1)}) fusion(s32[2048]{0:T(1024)S(1)} %iota.13), kind=kLoop, calls=%fused_computation.48 | loop fusion | flops 1835008 | bytes 1056768 | tf_op jit(solution)/shard_map/sin | solution.py:34
  30.2 1.1 fusion.23
  31.3 5.9 %table.1.table_hbm = bf16[2,2048,2048]{2,1,0:T(8,128)(2,1)S(1)} custom-call(f32[32,2048]{1,0:T(8,128)S(1)} %get-tuple-element.39.coarse_cos, f32[32,2048]{1,0:T(8,128)S(1)} %get-tuple-element.38.coarse_sin, f32[64,2048]{1,0:T(8,128)S(1)} %get-tuple-element.41.fine_cos, f32[64,2048]{1,0:T(8,128)S(1)} %get-tuple-element.40.fine_sin), custom_call_target="tpu_custom_call" | custom-call | flops 25165824 | bytes 16777216 | tf_op jit(solution)/shard_map/table/pallas_call | solution.py:39
  37.3 5.7 %copy-done = bf16[2,2048,2048]{2,1,0:T(8,128)(2,1)} copy-done((bf16[2,2048,2048]{2,1,0:T(8,128)(2,1)}, bf16[2,2048,2048]{2,1,0:T(8,128)(2,1)S(1)}, u32[]{:S(2)}) %copy-start) | copy-done | bytes 16777240
  45.0 1.1 slice.124
  46.0 9.2 %embed.1 = (bf16[2048,1024]{1,0:T(8,128)(2,1)S(1)}, bf16[2048,192]{1,0:T(8,128)(2,1)S(1)}) custom-call(s32[2048,8]{1,0:T(8,128)S(1)} %bitcast.32, bf16[1024,1024]{1,0:T(8,128)(2,1)S(1)} %dynamic-slice_dynamic-update-slice_fusion.used, bf16[1024,192]{1,0:T(8,128)(2,1)S(1)} %bitcast.33), custom_call_target="tpu_custom_call" | custom-call | tf_op jit(solution)/shard_map/embed/pallas_call | solution.py:82
  55.3 1.9 %copy-done.5 = bf16[2048,1024]{1,0:T(8,128)(2,1)} copy-done((bf16[2048,1024]{1,0:T(8,128)(2,1)}, bf16[2048,1024]{1,0:T(8,128)(2,1)S(1)}, u32[]{:S(2)}) %copy-start.5) | copy-done | bytes 4194328
  59.0 1.1 pad_maximum_fusion.4.gates
  60.1 1.3 %pad_maximum_fusion.signals = bf16[2048,256]{1,0:T(8,128)(2,1)} fusion(bf16[2048,64]{1,0:T(8,128)(2,1)S(1)} %fusion.6, bf16[2048,64]{1,0:T(8,128)(2,1)S(1)} %get-tuple-element.29, bf16[2048,128]{1,0:T(8,128)(2,1)S(1)} %copy-done.10), kind=kLoop, calls=%fused_computation.20 | loop fusion | flops 3145728 | bytes 2097152 | tf_op jit(solution)/shard_map/concatenate | solution.py:421
  61.4 24.0 %mixer.1 = (bf16[2048,128]{1,0:T(8,128)(2,1)}, bf16[2048,128]{1,0:T(8,128)(2,1)}, bf16[2048,256]{1,0:T(8,128)(2,1)}, bf16[2048,256]{1,0:T(8,128)(2,1)}, f32[8,128]{1,0:T(8,128)}) custom-call(bf16[2,2048,2048]{2,1,0:T(8,128)(2,1)} %copy-done, bf16[2048,256]{1,0:T(8,128)(2,1)} %pad_maximum_fusion.signals, bf16[2048,128]{1,0:T(8,128)(2,1)} %pad_maximum_fusion.4.gates), custom_call_target="tpu_custom_call" | custom-call | flops 10737418240 | bytes 16777216 | tf_op jit(solution)/shard_map/mixer/pallas_call | solution.py:285
  85.5 1.4 %fusion.5 = (bf16[2048,64]{1,0:T(8,128)(2,1)S(1)}, bf16[2048,64]{1,0:T(8,128)(2,1)S(1)}) fusion(bf16[2048,192]{1,0:T(8,128)(2,1)S(1)} %add_convert_fusion, bf16[2048,128]{1,0:T(8,128)(2,1)} %get-tuple-element.15, bf16[16,128,64]{2,1,0:T(8,128)(2,1)S(1)} %pad_maximum_fusion.3), kind=kLoop, calls=%fused_computation.17 | loop fusion | flops 917504 | bytes 1310720 | tf_op jit(solution)/shard_map/convert_element_type | solution.py:21
  87.1 1.4 %multiply_reduce_fusion.1 = (bf16[192]{0:T(256)(128)(2,1)S(1)}, bf16[192]{0:T(256)(128)(2,1)S(1)}, bf16[192]{0:T(256)(128)(2,1)S(1)}) fusion(f32[2048,192]{1,0:T(8,128)S(1)} %convert_element_type.78, bf16[2048,64]{1,0:T(8,128)(2,1)S(1)} %get-tuple-element.37, bf16[2048,64]{1,0:T(8,128)(2,1)S(1)} %bitcast.36, bf16[2048,64]{1,0:T(8,128)(2,1)S(1)} %slice.114, ...), kind=kLoop, calls=%fused_computation.10 | loop fusion | flops 5111232 | bytes 3146880 | tf_op jit(solution)/shard_map/reduce_sum | solution.py:432
  89.0 0.8 convert_element_type.90
  89.7 3.4 %convolution_convert_fusion = bf16[1024,192]{0,1:T(8,128)(2,1)S(1)} fusion(bf16[2048,1024]{1,0:T(8,128)(2,1)} %copy-done.5, f32[2048,192]{1,0:T(8,128)S(1)} %fusion.29, f32[192]{0:T(256)S(1)} %mul.133, f32[192]{0:T(256)S(1)} %mul.130, f32[192]{0:T(256)S(1)} %mul.115), kind=kOutput, calls=%fused_computation.16 | convolution fusion | flops 807862272 | bytes 6162688 | tf_op jit(solution)/shard_map/tr,tc->rc/dot_general | solution.py:434
  93.4 0.9 broadcast_in_dim.2
  94.3 1.3 %pad_maximum_fusion.2 = bf16[16,64,329]{2,1,0:T(8,128)(2,1)} fusion(bf16[16,64,9]{2,1,0:T(8,128)(2,1)S(1)} %broadcast_in_dim.2, bf16[16,64,64]{2,1,0:T(8,128)(2,1)S(1)} %get-tuple-element.35, bf16[16,64,64]{2,1,0:T(8,128)(2,1)S(1)} %get-tuple-element.34, bf16[16,64,192]{2,1,0:T(8,128)(2,1)S(1)} %bitcast.35), kind=kLoop, calls=%fused_computation.25 | loop fusion | flops 2695168 | bytes 1347584 | tf_op jit(solution)/shard_map/concatenate | solution.py:440
  95.5 6.0 %all-to-all-start.1 = ((bf16[16,64,329]{2,1,0:T(8,128)(2,1)}), bf16[16,64,329]{2,1,0:T(8,128)(2,1)S(1)}, u32[]{:S(2)}, u32[]{:S(2)}) async-start(bf16[16,64,329]{2,1,0:T(8,128)(2,1)} %pad_maximum_fusion.2), calls=%async_computation.1 | async-start | bytes 1572864 | tf_op jit(solution)/shard_map/all_to_all | solution.py:439
  101.6 5.8 %copy-done.1 = bf16[2,2048,2048]{2,1,0:T(8,128)(2,1)S(1)} copy-done((bf16[2,2048,2048]{2,1,0:T(8,128)(2,1)S(1)}, bf16[2,2048,2048]{2,1,0:T(8,128)(2,1)}, u32[]{:S(2)}) %copy-start.1) | copy-done | bytes 16777240
  107.4 4.3 %lags.1 = f32[2,64,2048]{2,1,0:T(8,128)} custom-call(bf16[2,2048,2048]{2,1,0:T(8,128)(2,1)S(1)} %copy-done.1, bf16[2048,256]{1,0:T(8,128)(2,1)S(1)} %copy-done.2, bf16[2048,256]{1,0:T(8,128)(2,1)S(1)} %copy-done.3, f32[8,128]{1,0:T(8,128)S(1)} %copy-done.4), custom_call_target="tpu_custom_call" | custom-call | flops 2147483648 | bytes 12582912 | tf_op jit(solution)/shard_map/lags/pallas_call | solution.py:318
  111.6 9.5 %all-to-all-done.1.got_ref = bf16[16,64,329]{2,1,0:T(8,128)(2,1)S(1)} async-done(((bf16[16,64,329]{2,1,0:T(8,128)(2,1)}), bf16[16,64,329]{2,1,0:T(8,128)(2,1)S(1)}, u32[]{:S(2)}, u32[]{:S(2)}) %all-to-all-start.1) | async-done | bytes 673824 | tf_op jit(solution)/shard_map/all_to_all | solution.py:439
  122.4 2.3 %unpack.1 = (bf16[128,1024]{1,0:T(8,128)(2,1)}, f32[64,3072]{1,0:T(8,128)}) custom-call(bf16[16,64,329]{2,1,0:T(8,128)(2,1)} %copy-done.8), custom_call_target="tpu_custom_call" | custom-call | tf_op jit(solution)/shard_map/unpack/pallas_call | solution.py:450
  (71 shorter events, 8.4 us)
Async XLA Ops:
  0.6 10.3 %copy-start.15 = (s32[8]{0:T(128)S(1)}, s32[8]{0:T(128)}, u32[]{:S(2)}) copy-start(s32[8]{0:T(128)} %param.8) | copy-start | bytes 100
  0.6 21.1 %copy-start.14 = (f32[3,3072]{1,0:T(4,128)S(1)}, f32[3,3072]{1,0:T(4,128)}, u32[]{:S(2)}) copy-start(f32[3,3072]{1,0:T(4,128)} %param.11) | copy-start | bytes 110596
  0.7 21.5 %copy-start.13 = (bf16[2,64,2048]{2,1,0:T(8,128)(2,1)S(1)}, bf16[2,64,2048]{2,1,0:T(8,128)(2,1)}, u32[]{:S(2)}) copy-start(bf16[2,64,2048]{2,1,0:T(8,128)(2,1)} %param.12) | copy-start | bytes 1572868
  4.4 39.3 %all-to-all-start = ((bf16[16,64,336]{2,1,0:T(8,128)(2,1)}), bf16[16,64,336]{2,1,0:T(8,128)(2,1)S(1)}, u32[]{:S(2)}, u32[]{:S(2)}) async-start(bf16[16,64,336]{2,1,0:T(8,128)(2,1)} %pack.1), calls=%async_computation | async-start | bytes 1572864 | tf_op jit(solution)/shard_map/all_to_all | solution.py:390
  31.3 11.7 %copy-start.9 = (bf16[1024,1024]{1,0:T(8,128)(2,1)S(1)}, bf16[1024,1024]{1,0:T(8,128)(2,1)}, u32[]{:S(2)}) copy-start(bf16[1024,1024]{1,0:T(8,128)(2,1)} %param.9) | copy-start | bytes 6291460
  37.2 5.7 %copy-start = (bf16[2,2048,2048]{2,1,0:T(8,128)(2,1)}, bf16[2,2048,2048]{2,1,0:T(8,128)(2,1)S(1)}, u32[]{:S(2)}) copy-start(bf16[2,2048,2048]{2,1,0:T(8,128)(2,1)S(1)} %table.1.table_hbm) | copy-start | bytes 50331652
  43.6 0.9 copy-start.6
  55.3 1.9 %copy-start.5 = (bf16[2048,1024]{1,0:T(8,128)(2,1)}, bf16[2048,1024]{1,0:T(8,128)(2,1)S(1)}, u32[]{:S(2)}) copy-start(bf16[2048,1024]{1,0:T(8,128)(2,1)S(1)} %get-tuple-element.13) | copy-start | bytes 12582916
  57.4 1.1 copy-start.7
  58.7 1.4 %copy-start.10 = (bf16[2048,128]{1,0:T(8,128)(2,1)S(1)}, bf16[2048,128]{1,0:T(8,128)(2,1)}, u32[]{:S(2)}) copy-start(bf16[2048,128]{1,0:T(8,128)(2,1)} %copy.42) | copy-start | bytes 1572868
  85.4 1.4 %copy-start.11 = (bf16[2048,128]{1,0:T(8,128)(2,1)S(1)}, bf16[2048,128]{1,0:T(8,128)(2,1)}, u32[]{:S(2)}) copy-start(bf16[2048,128]{1,0:T(8,128)(2,1)} %get-tuple-element.15) | copy-start | bytes 1572868
  85.4 1.6 %copy-start.12 = (bf16[2048,128]{1,0:T(8,128)(2,1)S(1)}, bf16[2048,128]{1,0:T(8,128)(2,1)}, u32[]{:S(2)}) copy-start(bf16[2048,128]{1,0:T(8,128)(2,1)} %get-tuple-element.16) | copy-start | bytes 1572868
  93.3 8.2 %copy-start.2 = (bf16[2048,256]{1,0:T(8,128)(2,1)S(1)}, bf16[2048,256]{1,0:T(8,128)(2,1)}, u32[]{:S(2)}) copy-start(bf16[2048,256]{1,0:T(8,128)(2,1)} %get-tuple-element.19.lag_re) | copy-start | bytes 3145732
  93.3 8.2 %copy-start.3 = (bf16[2048,256]{1,0:T(8,128)(2,1)S(1)}, bf16[2048,256]{1,0:T(8,128)(2,1)}, u32[]{:S(2)}) copy-start(bf16[2048,256]{1,0:T(8,128)(2,1)} %get-tuple-element.20.lag_im) | copy-start | bytes 3145732
  93.4 8.2 %copy-start.4 = (f32[8,128]{1,0:T(8,128)S(1)}, f32[8,128]{1,0:T(8,128)}, u32[]{:S(2)}) copy-start(f32[8,128]{1,0:T(8,128)} %get-tuple-element.21.ends) | copy-start | bytes 12292
  95.5 25.6 %all-to-all-start.1 = ((bf16[16,64,329]{2,1,0:T(8,128)(2,1)}), bf16[16,64,329]{2,1,0:T(8,128)(2,1)S(1)}, u32[]{:S(2)}, u32[]{:S(2)}) async-start(bf16[16,64,329]{2,1,0:T(8,128)(2,1)} %pad_maximum_fusion.2), calls=%async_computation.1 | async-start | bytes 1572864 | tf_op jit(solution)/shard_map/all_to_all | solution.py:439
  101.6 5.8 %copy-start.1 = (bf16[2,2048,2048]{2,1,0:T(8,128)(2,1)S(1)}, bf16[2,2048,2048]{2,1,0:T(8,128)(2,1)}, u32[]{:S(2)}) copy-start(bf16[2,2048,2048]{2,1,0:T(8,128)(2,1)} %copy-done) | copy-start | bytes 50331652
  121.1 1.3 %copy-start.8 = (bf16[16,64,329]{2,1,0:T(8,128)(2,1)}, bf16[16,64,329]{2,1,0:T(8,128)(2,1)S(1)}, u32[]{:S(2)}) copy-start(bf16[16,64,329]{2,1,0:T(8,128)(2,1)S(1)} %all-to-all-done.1.got_ref) | copy-start | bytes 2021380

commit v4 on v3

--- a/solution.py
+++ b/solution.py
@@ -45,7 +45,7 @@
         cost_estimate=pl.CostEstimate(
             flops=6 * half * half, bytes_accessed=4 * half * half, transcendentals=0
         ),
-        compiler_params=pltpu.CompilerParams(vmem_limit_bytes=24 << 20),
+        compiler_params=pltpu.CompilerParams(vmem_limit_bytes=VMEM),
         name="table",
     )(coarse_cos, coarse_sin, fine_cos, fine_sin)
 
@@ -389,13 +389,8 @@
     )(w_in, cotangent, narrow(token_ids))
     got = lax.all_to_all(sent, "tm", split_axis=0, concat_axis=0, tiled=True)
     table = dense_table(2 * length)
-    used = jnp.concatenate(
-        [
-            lax.dynamic_slice_in_dim(embed_table, field_offsets[field], CODES, 0)
-            for field in range(fields)
-        ],
-        axis=0,
-    )
+    used_rows = field_offsets[:, None] + jnp.arange(CODES, dtype=jnp.int32)[None, :]
+    used = jnp.take(embed_table, used_rows.reshape(-1), axis=0, mode="clip")
     filter_rows = filters.transpose(2, 0, 1).reshape(length, 2 * chans)
 
     def halves(start, count):

time: 126 us -> 128 us (1.016)
  between operations: 16.2 us -> 0.91 us
  Pallas kernels: 48 us -> 58.7 us
  other arithmetic: 12.1 us -> 17.4 us
  matrix products: 3.37 us -> 5.29 us
    pallas_call x1, Pallas kernels: 5.91 us -> 16.5 us  [dense_table(): pl.pallas_call(table_kernel, grid=(outer,), out_shape=jax.ShapeDtypeStruc...]
    gather x0 -> x1, local copies, waits for them, and re-layouts: none -> 5.34 us  [fast_local(): used = jnp.take(embed_table, used_rows.reshape(-1), axis=0, mode='clip')]
    unnamed x39 -> x30, local copies, waits for them, and re-layouts: 14.6 us -> 11.1 us
    dot_general x1, matrix products: 3.37 us -> 5.29 us  [fast_local(): jnp.einsum('tr,tc->rc', embedded, grad_proj, preferred_element_type=jnp.f...]
    sin x2, other arithmetic: 3.14 us -> 4.75 us  [cis(): return (jnp.cos(angle), jnp.sin(angle))]
    convert_element_type x2, other arithmetic: 0.62 us -> 1.95 us  [widen(): return array.astype(jnp.float32)]
  transfers between devices with their start and end apart: 2 -> 2, of which waited for: 1 -> 1; matrix products, arithmetic and copies ran while one was open for 5% -> 9% of each run, Pallas kernels for 8% -> 16%
where the time goes in v4:
time: 128 us; the launch traced here: 127 us
  Pallas kernels  58.7 us (46%)
  local copies, waits for them, and re-layouts  24.1 us (19%)
  other arithmetic  17.4 us (14%)
  starting transfers between devices  12.6 us (10%)
  waiting for transfers between devices  8.37 us (7%)
  matrix products  5.29 us (4%)
    pallas_call x1, Pallas kernels, fused_mixer(): pl.pallas_call(mixer_kernel, out_shape=(narrow_out, narrow_out, wide_out,...  24.1 us
    pallas_call x1, Pallas kernels, dense_table(): pl.pallas_call(table_kernel, grid=(outer,), out_shape=jax.ShapeDtypeStruc...  16.5 us
    unnamed x30, local copies, waits for them, and re-layouts  11.1 us
    pallas_call x1, Pallas kernels, embed(): pl.pallas_call(embed_kernel, grid=(length // block,), out_shape=(jax.Shap...  9.2 us
    all_to_all x1, waiting for transfers between devices, fast_local(): lax.all_to_all(jnp.concatenate([weight_terms.reshape(peers, chans, -1), m...  8.36 us
    all_to_all x1, starting transfers between devices, fast_local(): got = lax.all_to_all(sent, 'tm', split_axis=0, concat_axis=0, tiled=True)  6.61 us
    all_to_all x1, starting transfers between devices, fast_local(): lax.all_to_all(jnp.concatenate([weight_terms.reshape(peers, chans, -1), m...  6.02 us
    gather x1, local copies, waits for them, and re-layouts, fast_local(): used = jnp.take(embed_table, used_rows.reshape(-1), axis=0, mode='clip')  5.34 us
  transfers between devices with their start and end apart: 2, of which 1 were waited for; matrix products, arithmetic and copies ran while one was open for 9% of the time, Pallas kernels for 16%

profile of v4, /device:TPU:9, one launch (start us, length us, event | category | flops | bytes accessed | tf_op | source)
XLA Modules:
  0.0 127.4 jit_solution(14285888468582101872)
XLA Ops:
  2.2 2.2 %pack.1 = bf16[16,64,336]{2,1,0:T(8,128)(2,1)} custom-call(bf16[64,3072]{1,0:T(8,128)(2,1)} %w_ref.1, bf16[128,1024]{1,0:T(8,128)(2,1)} %cot_ref.1, bf16[128,8]{1,0:T(8,128)(2,1)} %copy.38.tok_ref), custom_call_target="tpu_custom_call" | custom-call | tf_op jit(solution)/shard_map/pack/pallas_call | solution.py:385
  4.5 6.6 %all-to-all-start = ((bf16[16,64,336]{2,1,0:T(8,128)(2,1)}), bf16[16,64,336]{2,1,0:T(8,128)(2,1)S(1)}, u32[]{:S(2)}, u32[]{:S(2)}) async-start(bf16[16,64,336]{2,1,0:T(8,128)(2,1)} %pack.1), calls=%async_computation | async-start | bytes 1572864 | tf_op jit(solution)/shard_map/all_to_all | solution.py:390
  12.5 5.3 %gather_fusion = bf16[1024,1024]{1,0:T(8,128)(2,1)} fusion(bf16[1024,1024]{1,0:T(8,128)(2,1)S(1)} %copy-done, s32[1024]{0:T(1024)S(1)} %bitcast_clamp_fusion), kind=kCustom, calls=%fused_computation | custom fusion | bytes 4198400 | tf_op jit(solution)/shard_map/jit(_take)/gather | solution.py:393
  17.9 1.9 %fusion.23 = (f32[32,2048]{1,0:T(8,128)}, f32[32,2048]{1,0:T(8,128)}) fusion(s32[2048]{0:T(1024)S(1)} %iota.17, s32[32]{0:T(128)S(1)} %iota_multiply_fusion), kind=kLoop, calls=%fused_computation.51 | loop fusion | flops 917504 | bytes 532608 | tf_op jit(solution)/shard_map/sin | solution.py:34
  19.8 2.9 %fusion.21 = (f32[64,2048]{1,0:T(8,128)}, f32[64,2048]{1,0:T(8,128)}) fusion(s32[2048]{0:T(1024)S(1)} %iota.17), kind=kLoop, calls=%fused_computation.49 | loop fusion | flops 1835008 | bytes 1056768 | tf_op jit(solution)/shard_map/sin | solution.py:34
  22.6 16.5 %table.1.table_hbm = bf16[2,2048,2048]{2,1,0:T(8,128)(2,1)} custom-call(f32[32,2048]{1,0:T(8,128)} %get-tuple-element.39.coarse_cos, f32[32,2048]{1,0:T(8,128)} %get-tuple-element.38.coarse_sin, f32[64,2048]{1,0:T(8,128)} %get-tuple-element.41.fine_cos, f32[64,2048]{1,0:T(8,128)} %get-tuple-element.40.fine_sin), custom_call_target="tpu_custom_call" | custom-call | flops 25165824 | bytes 16777216 | tf_op jit(solution)/shard_map/table/pallas_call | solution.py:39
  40.5 1.1 slice.94
  41.6 1.6 %copy-done.2 = bf16[1024,1024]{1,0:T(8,128)(2,1)S(1)} copy-done((bf16[1024,1024]{1,0:T(8,128)(2,1)S(1)}, bf16[1024,1024]{1,0:T(8,128)(2,1)}, u32[]{:S(2)}) %copy-start.2) | copy-done | bytes 2097176
  43.2 9.2 %embed.1 = (bf16[2048,1024]{1,0:T(8,128)(2,1)S(1)}, bf16[2048,192]{1,0:T(8,128)(2,1)S(1)}) custom-call(s32[2048,8]{1,0:T(8,128)S(1)} %bitcast.26, bf16[1024,1024]{1,0:T(8,128)(2,1)S(1)} %copy-done.2, bf16[1024,192]{1,0:T(8,128)(2,1)S(1)} %bitcast.27), custom_call_target="tpu_custom_call" | custom-call | tf_op jit(solution)/shard_map/embed/pallas_call | solution.py:82
  52.4 1.9 %copy-done.6 = bf16[2048,1024]{1,0:T(8,128)(2,1)} copy-done((bf16[2048,1024]{1,0:T(8,128)(2,1)}, bf16[2048,1024]{1,0:T(8,128)(2,1)S(1)}, u32[]{:S(2)}) %copy-start.6) | copy-done | bytes 4194328
  57.2 1.3 %pad_maximum_fusion.signals = bf16[2048,256]{1,0:T(8,128)(2,1)} fusion(bf16[2048,64]{1,0:T(8,128)(2,1)S(1)} %fusion.6, bf16[2048,64]{1,0:T(8,128)(2,1)S(1)} %get-tuple-element.29, bf16[2048,128]{1,0:T(8,128)(2,1)S(1)} %copy-done.9), kind=kLoop, calls=%fused_computation.21 | loop fusion | flops 3145728 | bytes 2097152 | tf_op jit(solution)/shard_map/concatenate | solution.py:416
  58.5 24.1 %mixer.1 = (bf16[2048,128]{1,0:T(8,128)(2,1)}, bf16[2048,128]{1,0:T(8,128)(2,1)}, bf16[2048,256]{1,0:T(8,128)(2,1)}, bf16[2048,256]{1,0:T(8,128)(2,1)}, f32[8,128]{1,0:T(8,128)}) custom-call(bf16[2,2048,2048]{2,1,0:T(8,128)(2,1)} %table.1.table_hbm, bf16[2048,256]{1,0:T(8,128)(2,1)} %pad_maximum_fusion.signals, bf16[2048,128]{1,0:T(8,128)(2,1)} %pad_maximum_fusion.4.gates), custom_call_target="tpu_custom_call" | custom-call | flops 10737418240 | bytes 16777216 | tf_op jit(solution)/shard_map/mixer/pallas_call | solution.py:285
  82.7 1.4 %fusion.5 = (bf16[2048,64]{1,0:T(8,128)(2,1)S(1)}, bf16[2048,64]{1,0:T(8,128)(2,1)S(1)}) fusion(bf16[2048,192]{1,0:T(8,128)(2,1)S(1)} %add_convert_fusion, bf16[2048,128]{1,0:T(8,128)(2,1)} %get-tuple-element.15, bf16[16,128,64]{2,1,0:T(8,128)(2,1)S(1)} %pad_maximum_fusion.3), kind=kLoop, calls=%fused_computation.18 | loop fusion | flops 917504 | bytes 1310720 | tf_op jit(solution)/shard_map/convert_element_type | solution.py:21
  84.3 1.4 %multiply_reduce_fusion.1 = (bf16[192]{0:T(256)(128)(2,1)S(1)}, bf16[192]{0:T(256)(128)(2,1)S(1)}, bf16[192]{0:T(256)(128)(2,1)S(1)}) fusion(f32[2048,192]{1,0:T(8,128)S(1)} %convert_element_type.78, bf16[2048,64]{1,0:T(8,128)(2,1)S(1)} %get-tuple-element.37, bf16[2048,64]{1,0:T(8,128)(2,1)S(1)} %bitcast.30, bf16[2048,64]{1,0:T(8,128)(2,1)S(1)} %slice.82, ...), kind=kLoop, calls=%fused_computation.11 | loop fusion | flops 5111232 | bytes 3146880 | tf_op jit(solution)/shard_map/reduce_sum | solution.py:427
  85.6 1.8 %fusion.26 = f32[2048,192]{1,0:T(8,128)} fusion(bf16[2048,64]{1,0:T(8,128)(2,1)S(1)} %get-tuple-element.37, bf16[2048,64]{1,0:T(8,128)(2,1)S(1)} %bitcast.31, bf16[2048,64]{1,0:T(8,128)(2,1)S(1)} %slice.82), kind=kLoop, calls=%fused_computation.61 | loop fusion | flops 2359296 | bytes 2359296 | tf_op jit(solution)/shard_map/convert_element_type | solution.py:17
  88.4 5.3 %convolution_convert_fusion = bf16[1024,192]{0,1:T(8,128)(2,1)S(1)} fusion(bf16[2048,1024]{1,0:T(8,128)(2,1)} %copy-done.6, f32[2048,192]{1,0:T(8,128)} %fusion.26, f32[192]{0:T(256)S(1)} %mul.133, f32[192]{0:T(256)S(1)} %mul.130, f32[192]{0:T(256)S(1)} %mul.115), kind=kOutput, calls=%fused_computation.17 | convolution fusion | flops 807862272 | bytes 6162688 | tf_op jit(solution)/shard_map/tr,tc->rc/dot_general | solution.py:429
  94.7 2.5 %pad_maximum_fusion.2 = bf16[16,64,329]{2,1,0:T(8,128)(2,1)} fusion(bf16[16,64,9]{2,1,0:T(8,128)(2,1)S(1)} %broadcast_in_dim.3, bf16[16,64,64]{2,1,0:T(8,128)(2,1)} %get-tuple-element.35, bf16[16,64,64]{2,1,0:T(8,128)(2,1)S(1)} %get-tuple-element.34, bf16[16,64,192]{2,1,0:T(8,128)(2,1)} %bitcast.29), kind=kLoop, calls=%fused_computation.26 | loop fusion | flops 2695168 | bytes 1347584 | tf_op jit(solution)/shard_map/concatenate | solution.py:435
  97.2 6.0 %all-to-all-start.1 = ((bf16[16,64,329]{2,1,0:T(8,128)(2,1)}), bf16[16,64,329]{2,1,0:T(8,128)(2,1)}, u32[]{:S(2)}, u32[]{:S(2)}) async-start(bf16[16,64,329]{2,1,0:T(8,128)(2,1)} %pad_maximum_fusion.2), calls=%async_computation.1 | async-start | bytes 1572864 | tf_op jit(solution)/shard_map/all_to_all | solution.py:434
  103.2 5.8 %copy-done.1 = bf16[2,2048,2048]{2,1,0:T(8,128)(2,1)S(1)} copy-done((bf16[2,2048,2048]{2,1,0:T(8,128)(2,1)S(1)}, bf16[2,2048,2048]{2,1,0:T(8,128)(2,1)}, u32[]{:S(2)}) %copy-start.1) | copy-done | bytes 16777240
  109.0 1.2 copy-done.4
  110.2 4.3 %lags.1 = f32[2,64,2048]{2,1,0:T(8,128)} custom-call(bf16[2,2048,2048]{2,1,0:T(8,128)(2,1)S(1)} %copy-done.1, bf16[2048,256]{1,0:T(8,128)(2,1)S(1)} %copy-done.3, bf16[2048,256]{1,0:T(8,128)(2,1)S(1)} %copy-done.4, f32[8,128]{1,0:T(8,128)S(1)} %copy-done.5), custom_call_target="tpu_custom_call" | custom-call | flops 2147483648 | bytes 12582912 | tf_op jit(solution)/shard_map/lags/pallas_call | solution.py:318
  114.5 8.4 %all-to-all-done.1.got_ref = bf16[16,64,329]{2,1,0:T(8,128)(2,1)} async-done(((bf16[16,64,329]{2,1,0:T(8,128)(2,1)}), bf16[16,64,329]{2,1,0:T(8,128)(2,1)}, u32[]{:S(2)}, u32[]{:S(2)}) %all-to-all-start.1) | async-done | bytes 673824 | tf_op jit(solution)/shard_map/all_to_all | solution.py:434
  122.9 1.1 slice_convert_fusion
  125.1 2.3 %unpack.1 = (bf16[128,1024]{1,0:T(8,128)(2,1)}, f32[64,3072]{1,0:T(8,128)}) custom-call(bf16[16,64,329]{2,1,0:T(8,128)(2,1)} %all-to-all-done.1.got_ref), custom_call_target="tpu_custom_call" | custom-call | tf_op jit(solution)/shard_map/unpack/pallas_call | solution.py:445
  (62 shorter events, 10.4 us)
Async XLA Ops:
  0.6 11.9 %copy-start = (bf16[1024,1024]{1,0:T(8,128)(2,1)S(1)}, bf16[1024,1024]{1,0:T(8,128)(2,1)}, u32[]{:S(2)}) copy-start(bf16[1024,1024]{1,0:T(8,128)(2,1)} %param.9) | copy-start | bytes 6291460
  0.6 10.4 %copy-start.13 = (f32[3,3072]{1,0:T(4,128)S(1)}, f32[3,3072]{1,0:T(4,128)}, u32[]{:S(2)}) copy-start(f32[3,3072]{1,0:T(4,128)} %param.11) | copy-start | bytes 110596
  0.7 10.8 %copy-start.12 = (bf16[2,64,2048]{2,1,0:T(8,128)(2,1)S(1)}, bf16[2,64,2048]{2,1,0:T(8,128)(2,1)}, u32[]{:S(2)}) copy-start(bf16[2,64,2048]{2,1,0:T(8,128)(2,1)} %param.12) | copy-start | bytes 1572868
  2.2 10.2 %copy-start.14 = (s32[8]{0:T(128)S(1)}, s32[8]{0:T(128)}, u32[]{:S(2)}) copy-start(s32[8]{0:T(128)} %param.8) | copy-start | bytes 100
  4.5 34.7 %all-to-all-start = ((bf16[16,64,336]{2,1,0:T(8,128)(2,1)}), bf16[16,64,336]{2,1,0:T(8,128)(2,1)S(1)}, u32[]{:S(2)}, u32[]{:S(2)}) async-start(bf16[16,64,336]{2,1,0:T(8,128)(2,1)} %pack.1), calls=%async_computation | async-start | bytes 1572864 | tf_op jit(solution)/shard_map/all_to_all | solution.py:390
  39.2 0.9 copy-start.7
  41.6 1.6 %copy-start.2 = (bf16[1024,1024]{1,0:T(8,128)(2,1)S(1)}, bf16[1024,1024]{1,0:T(8,128)(2,1)}, u32[]{:S(2)}) copy-start(bf16[1024,1024]{1,0:T(8,128)(2,1)} %gather_fusion) | copy-start | bytes 6291460
  52.4 1.9 %copy-start.6 = (bf16[2048,1024]{1,0:T(8,128)(2,1)}, bf16[2048,1024]{1,0:T(8,128)(2,1)S(1)}, u32[]{:S(2)}) copy-start(bf16[2048,1024]{1,0:T(8,128)(2,1)S(1)} %get-tuple-element.13) | copy-start | bytes 12582916
  54.5 1.1 copy-start.8
  55.8 1.4 %copy-start.9 = (bf16[2048,128]{1,0:T(8,128)(2,1)S(1)}, bf16[2048,128]{1,0:T(8,128)(2,1)}, u32[]{:S(2)}) copy-start(bf16[2048,128]{1,0:T(8,128)(2,1)} %copy.42) | copy-start | bytes 1572868
  82.7 1.4 %copy-start.10 = (bf16[2048,128]{1,0:T(8,128)(2,1)S(1)}, bf16[2048,128]{1,0:T(8,128)(2,1)}, u32[]{:S(2)}) copy-start(bf16[2048,128]{1,0:T(8,128)(2,1)} %get-tuple-element.15) | copy-start | bytes 1572868
  82.7 1.6 %copy-start.11 = (bf16[2048,128]{1,0:T(8,128)(2,1)S(1)}, bf16[2048,128]{1,0:T(8,128)(2,1)}, u32[]{:S(2)}) copy-start(bf16[2048,128]{1,0:T(8,128)(2,1)} %get-tuple-element.16) | copy-start | bytes 1572868
  94.7 8.5 %copy-start.3 = (bf16[2048,256]{1,0:T(8,128)(2,1)S(1)}, bf16[2048,256]{1,0:T(8,128)(2,1)}, u32[]{:S(2)}) copy-start(bf16[2048,256]{1,0:T(8,128)(2,1)} %get-tuple-element.19.lag_re) | copy-start | bytes 3145732
  94.7 8.5 %copy-start.5 = (f32[8,128]{1,0:T(8,128)S(1)}, f32[8,128]{1,0:T(8,128)}, u32[]{:S(2)}) copy-start(f32[8,128]{1,0:T(8,128)} %get-tuple-element.21.ends) | copy-start | bytes 12292
  97.2 25.7 %all-to-all-start.1 = ((bf16[16,64,329]{2,1,0:T(8,128)(2,1)}), bf16[16,64,329]{2,1,0:T(8,128)(2,1)}, u32[]{:S(2)}, u32[]{:S(2)}) async-start(bf16[16,64,329]{2,1,0:T(8,128)(2,1)} %pad_maximum_fusion.2), calls=%async_computation.1 | async-start | bytes 1572864 | tf_op jit(solution)/shard_map/all_to_all | solution.py:434
  103.2 5.8 %copy-start.1 = (bf16[2,2048,2048]{2,1,0:T(8,128)(2,1)S(1)}, bf16[2,2048,2048]{2,1,0:T(8,128)(2,1)}, u32[]{:S(2)}) copy-start(bf16[2,2048,2048]{2,1,0:T(8,128)(2,1)} %table.1.table_hbm) | copy-start | bytes 50331652
  109.0 1.2 copy-start.4
